TPU v7x, 256 devices: a whole 4x4x8 slice. The times are simulated.
256 devices in a mesh: dp: 32 (over x, z), feat: 8 (over y, core).
Axes of the slice: x: 4, y: 4, z: 8, core: 2. Of those that a mesh axis runs over, the one named last changes fastest.
Arguments:
- hidden_first: bfloat16 [2048, 4096], P('dp', 'feat'), may hold values from -6 to 6
- hidden_second: bfloat16 [2048, 4096], P('dp', 'feat'), may hold values from -11 to 11
- weight: bfloat16 [4096, 8192], P('dp', 'feat'), may hold values from -0.09375 to 0.09375
Outputs:
- total_loss: float32 [], replicated
- grad_weight: bfloat16 [4096, 8192], P('dp', 'feat')
- grad_first: bfloat16 [2048, 4096], P('dp', 'feat')
- grad_second: bfloat16 [2048, 4096], P('dp', 'feat')
All inputs are finite; a program needn't handle non-finite values.
Results may differ from a plain program's by a relative error of at most 0.015.
Values may be sent and summed in bfloat16 or wider, within the bound.
No kernel may reach another device: no remote copies, remote signals or barrier semaphores. Data moves between devices by JAX's collectives and lax.ppermute only.
A program may use at most 64 MiB of HBM per device.

v0:
```python
import functools

import jax
import jax.numpy as jnp
from jax import lax
from jax.experimental import pallas as pl
from jax.experimental.pallas import tpu as pltpu
from jax.sharding import Mesh, PartitionSpec as P


BF = jnp.bfloat16
F32 = jnp.float32
NX, NZ, NY, NC = 4, 8, 4, 2
HALF = NZ // 2
CHIPS = ("x", "y")
SMEM = pltpu.SMEM
STAT = 16


def swap_core(v):
    return lax.ppermute(v, "c", [(0, 1), (1, 0)])


def hop(v, k):
    return lax.ppermute(v, "z", [(i, (i + k) % NZ) for i in range(NZ)])


def exchange(v, axes):
    return lax.all_to_all(v, axes, split_axis=0, concat_axis=0, tiled=True)


def copies(v, n):
    return jnp.broadcast_to(v[None], (n,) + v.shape)


def ring_blocks(v):
    right, left = [v], [v]
    for _ in range(1, HALF):
        right.append(hop(right[-1], 1))
        left.append(hop(left[-1], -1))
    half = v.shape[0] // 2
    far = (hop(right[-1][:half], 1), hop(left[-1][half:], -1))
    return left[1:], right[:0:-1], far


def ring_pieces(first, second):
    got = [[None, None] for _ in range(NZ)]
    got[0] = [first, second]
    for k in range(1, HALF + 1):
        for p in (0, 1):
            if k < HALF or p == 0:
                got[-k % NZ][p] = hop(got[(1 - k) % NZ][p], 1)
            if k < HALF or p == 1:
                got[k][p] = hop(got[k - 1][p], -1)
    return got


def ring_sum(terms, right, left):
    for d in range(HALF - 1, 0, -1):
        right, left = lax.optimization_barrier((right, left))
        right, left = right.astype(F32), left.astype(F32)
        if d == HALF - 1:
            low, high = jnp.zeros(left.shape, F32), jnp.zeros(right.shape, F32)
            right = jnp.concatenate([right, low], axis=0)
            left = jnp.concatenate([high, left], axis=0)
        right = hop((terms[d].astype(F32) + right).astype(BF), 1)
        left = hop((terms[NZ - d].astype(F32) + left).astype(BF), -1)
    return terms[0].astype(F32) + right.astype(F32) + left.astype(F32)


def split3(v):
    hi = v.astype(BF).astype(F32)
    mid = (v - hi).astype(BF).astype(F32)
    return [hi, mid, v - hi - mid]


def dot(a, b, ca, cb):
    return lax.dot_general(a, b, (((ca,), (cb,)), ((), ())), preferred_element_type=F32)


def fixed(shape):
    return pl.BlockSpec(shape, lambda j: (0,) * len(shape))


def at_dim(shape, dim):
    return pl.BlockSpec(shape, lambda j: tuple(j if d == dim else 0 for d in range(len(shape))))


def flat_rows(ref):
    nx, _, nv, rows, width = ref.shape
    return ref[:, 0].reshape(nx * nv * rows, width)


def views_kernel(place_ref, own_ref, oth_ref, *refs):
    w_refs, refs = refs[:7], refs[7:]
    far_a, far_b, kept_ref, sent_ref, cen_ref, mine_ref, theirs_ref, stat_ref, w_ref, acc = refs
    step = pl.program_id(0)
    core = place_ref[0]
    zi = place_ref[1]
    nx, _, nv, rows, kpart = own_ref.shape
    sub = acc.shape[1]
    for k, ref in zip((0, 1, 2, 3, 5, 6, 7), w_refs):
        w_ref[lax.rem(zi + k, NZ)] = ref[0]
    w_ref[lax.rem(zi + HALF, NZ)] = jnp.where(step < NY // 2, far_a[0], far_b[0])
    w_own = w_ref[pl.ds(core * HALF, HALF)].reshape(kpart, sub)
    w_oth = w_ref[pl.ds((1 - core) * HALF, HALF)].reshape(kpart, sub)
    kept_ref[0] = w_own
    sent_ref[0] = w_oth
    term = dot(flat_rows(own_ref), w_own, 1, 0) + dot(flat_rows(oth_ref), w_oth, 1, 0)

    @pl.when(step == 0)
    def _():
        acc[...] = term

    @pl.when(step > 0)
    def _():
        acc[...] += term

    @pl.when(step == pl.num_programs(0) - 1)
    def _():
        means, tails = [], []
        for v in range(nv):
            blocks = [acc[(a * nv + v) * rows : (a * nv + v + 1) * rows] for a in range(nx)]
            mean = sum(jnp.sum(block, axis=0, keepdims=True) for block in blocks) / (nx * rows * 1.0)
            means.append(mean)
            total = jnp.zeros_like(mean)
            for a in range(nx):
                block = blocks[a] - mean
                cen_ref[v, a * rows : (a + 1) * rows] = block
                total = total + jnp.sum(block * block, axis=0, keepdims=True)
            pad = jnp.zeros((STAT - 6, sub), F32)
            tails.append(jnp.concatenate(split3(mean) + split3(total) + [pad], axis=0).astype(BF))
        stat_ref[...] = jnp.concatenate(means + [jnp.zeros((6, sub), F32)], axis=0)
        data = [cen_ref[v].astype(BF) for v in range(nv)]
        for ref, same in ((mine_ref, core == 0), (theirs_ref, core == 1)):
            ref[:STAT] = jnp.where(same, tails[0], tails[1])
            ref[STAT:] = jnp.where(same, data[0], data[1])


def gram_kernel(scale_each, diff_ref, *refs):
    pieces, (all_ref, gram_ref, stat_ref) = refs[: 2 * NZ], refs[2 * NZ :]
    top = pieces[0].shape[0] - STAT
    blk = top + pieces[1].shape[0]
    stats = [pieces[2 * k][:STAT].astype(F32) for k in range(NZ)]
    means = [s[0:1] + s[1:2] + s[2:3] for s in stats]
    center = sum(means) / (NZ * 1.0)
    total = sum(s[3:4] + s[4:5] + s[5:6] for s in stats)
    for k in range(NZ):
        move = means[k] - center
        total = total + blk * (move * move)
        all_ref[k * blk : k * blk + top] = (pieces[2 * k][STAT:].astype(F32) + move).astype(BF)
        all_ref[k * blk + top : (k + 1) * blk] = (pieces[2 * k + 1][...].astype(F32) + move).astype(BF)
        gram_ref[:, k * blk : (k + 1) * blk] = dot(
            all_ref[:blk], all_ref[k * blk : (k + 1) * blk], 1, 1
        ).astype(BF)
    variance = total / (NZ * blk - 1.0)
    pad = jnp.zeros((6, total.shape[1]), F32)
    stat_ref[...] = jnp.concatenate([variance, means[0] - center, pad], axis=0)
    hinge = jnp.maximum(1.0 - jnp.sqrt(variance + 0.0001), 0.0)
    share = diff_ref[...] + scale_each * jnp.sum(25.0 * hinge - variance * variance, axis=1, keepdims=True)
    extra = gram_ref.shape[1] - NZ * blk
    row = lax.broadcasted_iota(jnp.int32, (blk, extra), 0)
    lane = lax.broadcasted_iota(jnp.int32, (blk, extra), 1)
    lead = lax.rem(row, blk // (NX * NY)) == 0
    gram_ref[:, NZ * blk :] = in_lanes(share, lane, 0, lead).astype(BF)


def in_lanes(value, lane, start, keep):
    out = jnp.zeros(lane.shape, F32)
    for n, term in enumerate(split3(value)):
        out = jnp.where(keep & (lane == start + n), term, out)
    return out


def weight_kernel(place_ref, own_ref, oth_ref, g_ref, share_ref, out_ref):
    step = pl.program_id(0)
    core = place_ref[0]
    zi = place_ref[1]
    rows = NY * (own_ref.shape[4] // HALF)
    kz = rows // NY
    for ref, lead in ((own_ref, core), (oth_ref, 1 - core)):
        term = dot(flat_rows(ref), g_ref[...], 0, 0).astype(BF)
        for q in range(HALF):
            k = lax.rem(lead * HALF + q - zi + NZ, NZ)
            out_ref[k, pl.ds(pl.multiple_of(step * kz, kz), kz)] = term[q * kz : (q + 1) * kz]

    @pl.when(step == 0)
    def _():
        row = lax.broadcasted_iota(jnp.int32, (STAT, out_ref.shape[2]), 0)
        lane = lax.broadcasted_iota(jnp.int32, (STAT, out_ref.shape[2]), 1)
        tail = in_lanes(share_ref[...], lane, 3 * zi, row == 0).astype(BF)
        for k in range(NZ):
            out_ref[k, rows:] = tail


def far_kernel(place_ref, own_ref, oth_ref, g_ref, share_ref, a_ref, b_ref):
    step = pl.program_id(0)
    core = place_ref[0]
    zi = place_ref[1]
    kz = own_ref.shape[4]
    mine = 1 - zi // HALF == core
    block = jnp.where(mine, flat_rows(own_ref).astype(F32), flat_rows(oth_ref).astype(F32)).astype(BF)
    term = dot(block, g_ref[...], 0, 0).astype(BF)
    place = pl.ds(pl.multiple_of(lax.rem(step, NY // 2) * kz, kz), kz)

    @pl.when(step < NY // 2)
    def _():
        a_ref[place] = term

    @pl.when(step >= NY // 2)
    def _():
        b_ref[place] = term

    @pl.when(step == 0)
    def _():
        row = lax.broadcasted_iota(jnp.int32, (STAT, b_ref.shape[1]), 0)
        lane = lax.broadcasted_iota(jnp.int32, (STAT, b_ref.shape[1]), 1)
        b_ref[NY // 2 * kz :] = in_lanes(share_ref[...], lane, 3 * zi, row == 0).astype(BF)


def input_kernel(own_ref, oth_ref, kept_ref, recv_ref, out_ref):
    term = dot(own_ref[...], kept_ref[0], 1, 1) + dot(oth_ref[...], recv_ref[0], 1, 1)
    out_ref[0] = term.astype(BF)


def on_device(hidden_first, hidden_second, weight):
    core = lax.axis_index("c")
    place = jnp.stack([core, lax.axis_index("z")]).astype(jnp.int32)
    first = core == 0
    rows, kpart = hidden_first.shape
    kz, cols = weight.shape
    total_rows = rows * NX * NZ * 1.0
    full_width = cols * NY * NC * 1.0
    blk = rows * NX
    flat = 2 * blk
    sub = cols // NX
    hshape = (NX, NY, 2, rows, kpart)
    hblock = (NX, 1, 2, rows, kpart)
    smem = pl.BlockSpec(memory_space=SMEM)
    shape = jax.ShapeDtypeStruct

    w_parts = exchange(jnp.stack([weight[:, k * sub : (k + 1) * sub] for k in range(NX)]), "x")
    moved = copies(jnp.stack([hidden_first, hidden_second]), NX * NY)
    moved, w_parts = lax.optimization_barrier((moved, w_parts))
    h_own = exchange(moved, CHIPS).reshape(hshape)
    after, before, (far_a, far_b) = ring_blocks(w_parts)
    h_own, _, _ = lax.optimization_barrier((h_own, after[-1], before[0]))
    h_oth = swap_core(h_own)

    block_spec = at_dim((1, kz, sub), 0)
    w_kept, w_sent, cen, mine, theirs, stats = pl.pallas_call(
        views_kernel,
        grid=(NY,),
        in_specs=[smem, at_dim(hblock, 1), at_dim(hblock, 1)]
        + [block_spec] * 7
        + [
            pl.BlockSpec((1, kz, sub), lambda j: (jnp.minimum(j, NX // 2 - 1), 0, 0)),
            pl.BlockSpec((1, kz, sub), lambda j: (jnp.maximum(j - NX // 2, 0), 0, 0)),
        ],
        out_specs=[
            at_dim((1, kpart, sub), 0),
            at_dim((1, kpart, sub), 0),
            fixed((2, blk, sub)),
            fixed((blk + STAT, sub)),
            fixed((blk + STAT, sub)),
            fixed((8, sub)),
        ],
        out_shape=[
            shape((NY, kpart, sub), BF),
            shape((NY, kpart, sub), BF),
            shape((2, blk, sub), F32),
            shape((blk + STAT, sub), BF),
            shape((blk + STAT, sub), BF),
            shape((8, sub), F32),
        ],
        scratch_shapes=[pltpu.VMEM((NZ, kz, sub), BF), pltpu.VMEM((flat, sub), F32)],
        name="views",
    )(place, h_own, h_oth, w_parts, *after, *before, far_a, far_b)

    local = jnp.concatenate([mine, swap_core(theirs)], axis=1)
    got = ring_pieces(local[: STAT + blk // 2], local[STAT + blk // 2 :])

    w_recv = swap_core(w_sent)
    difference = cen[0] - cen[1] + (stats[0] - stats[1])[None, :]
    diff_share = (25.0 * jnp.sum(difference * difference) / (total_rows * full_width)).reshape(1, 1)

    wide = NZ * blk + 128
    flat_got = [piece for pair in got for piece in pair]
    whole = lambda s: pl.BlockSpec(s, lambda: (0,) * len(s))
    gathered, gram_part, view_stats = pl.pallas_call(
        functools.partial(gram_kernel, 1.0 / (full_width * NZ)),
        in_specs=[whole((1, 1))] + [whole(piece.shape) for piece in flat_got],
        out_specs=[whole((NZ * blk, 2 * sub)), whole((blk, wide)), whole((8, 2 * sub))],
        out_shape=[
            shape((NZ * blk, 2 * sub), BF),
            shape((blk, wide), BF),
            shape((8, 2 * sub), F32),
        ],
        name="gram",
    )(diff_share, *flat_got)

    stats_own = view_stats[:, :sub]
    stats_back = swap_core(view_stats[:, sub:])
    both_stats = jnp.stack(
        [jnp.where(first, stats_own, stats_back), jnp.where(first, stats_back, stats_own)]
    )
    variance = both_stats[:, 0]
    centered = cen + both_stats[:, 1][:, None, :]
    deviation = jnp.sqrt(variance + 0.0001)

    pieces = exchange(gram_part.reshape(NX * NY, blk // (NX * NY), wide), CHIPS)
    gram_rows = jnp.sum(pieces[:, :, : NZ * blk].astype(F32), axis=0).astype(BF)
    share = jnp.sum(pieces[:, :, NZ * blk :].astype(F32))
    gram_rows, share, variance, w_recv = lax.optimization_barrier((gram_rows, share, variance, w_recv))
    gram_half = exchange(copies(gram_rows, NX * NY), CHIPS).reshape(blk, NZ * blk)
    squares = gram_half.astype(F32)
    share = (share + jnp.sum(squares * squares) / ((total_rows - 1.0) ** 2 * full_width)).reshape(1, 1)
    spread_view = dot(gram_half, gathered, 1, 0)
    spread_own = spread_view[:, :sub]
    spread_back = swap_core(spread_view[:, sub:])
    spread = jnp.stack(
        [jnp.where(first, spread_own, spread_back), jnp.where(first, spread_back, spread_own)]
    )

    inv_grad = 50.0 / 256.0 * jnp.stack([difference, -difference])
    binding = (deviation < 1.0).astype(F32)
    hinge_grad = (
        -(25.0 * total_rows / (256.0 * (total_rows - 1.0)))
        * (binding / deviation)[:, None, :]
        * centered
    )
    cov_grad = (
        4.0
        * total_rows
        / 256.0
        * (spread / (total_rows - 1.0) ** 2 - variance[:, None, :] * centered / (total_rows - 1.0))
    )
    grad_views = (inv_grad + hinge_grad + cov_grad).astype(BF)
    grads = grad_views.reshape(2, NX, rows, sub).transpose(1, 0, 2, 3).reshape(flat, sub)

    far_block = pl.BlockSpec((NX, 1, 2, rows, kz), lambda j, place: (0, j, 0, 0, lax.rem(place[1], HALF)))
    held = lambda s: pl.BlockSpec(s, lambda j, place: (0,) * len(s))
    half = NX // 2 * kz
    far_right, far_left = pl.pallas_call(
        far_kernel,
        grid_spec=pltpu.PrefetchScalarGridSpec(
            num_scalar_prefetch=1,
            grid=(NY,),
            in_specs=[far_block, far_block, held((flat, sub)), held((1, 1))],
            out_specs=[held((half, sub)), held((half + STAT, sub))],
        ),
        out_shape=[shape((half, sub), BF), shape((half + STAT, sub), BF)],
        name="far_terms",
    )(place, h_own, h_oth, grads, share)
    right = hop(far_right, 1)
    left = hop(far_left, -1)

    later, _, _ = lax.optimization_barrier((grads, far_right, far_left))
    input_part = pl.pallas_call(
        input_kernel,
        grid=(NY,),
        in_specs=[fixed((flat, sub)), fixed((flat, sub)), at_dim((1, kpart, sub), 0), at_dim((1, kpart, sub), 0)],
        out_specs=at_dim((1, flat, kpart), 0),
        out_shape=shape((NY, flat, kpart), BF),
        name="input_terms",
    )(later, swap_core(grads), w_kept, w_recv)
    input_parts = exchange(input_part.reshape(NX * NY, 2, rows, kpart), ("y", "x"))

    later, _ = lax.optimization_barrier((later, input_part))
    terms = NX * kz + STAT
    weight_part = pl.pallas_call(
        weight_kernel,
        grid=(NY,),
        in_specs=[smem, at_dim(hblock, 1), at_dim(hblock, 1), fixed((flat, sub)), fixed((1, 1))],
        out_specs=fixed((NZ, terms, sub)),
        out_shape=shape((NZ, terms, sub), BF),
        name="weight_terms",
    )(place, h_own, h_oth, later, share)

    weight_sum = ring_sum(weight_part, right, left)
    loss_rows = weight_sum[NX * kz :]
    weight_sum = weight_sum[: NX * kz].astype(BF).reshape(NX, kz, sub)
    weight_sum, loss_rows, input_parts = lax.optimization_barrier((weight_sum, loss_rows, input_parts))
    loss_part = jnp.sum(loss_rows).reshape(1, 1)
    blocks = exchange(weight_sum, "x")
    input_grads = jnp.sum(input_parts.astype(F32), axis=0).astype(BF)
    grad_weight = jnp.concatenate([blocks[k] for k in range(NX)], axis=1)
    total_loss = (loss_part + swap_core(loss_part))[0, 0]
    return (total_loss, grad_weight, input_grads[0], input_grads[1])


def solution(mesh):
    grid = Mesh(mesh.devices.reshape(NX, NZ, NY, NC), ("x", "z", "y", "c"))
    placed = P(("x", "z"), ("y", "c"))

    return jax.shard_map(
        on_device,
        mesh=grid,
        in_specs=(placed, placed, placed),
        out_specs=(P(), placed, placed, placed),
        check_vma=False,
    )
```

profile of v0, /device:TPU:8, one launch (start us, length us, event | category | flops | bytes accessed | tf_op | source)
XLA Modules:
  0.0 220.6 jit_solution(4835268673280093541)
XLA Ops:
  2.3 4.3 %all-to-all-start = ((bf16[4,128,256]{2,1,0:T(8,128)(2,1)}), bf16[4,128,256]{2,1,0:T(8,128)(2,1)S(1)}, u32[]{:S(2)}, u32[]{:S(2)}) async-start(bf16[4,128,256]{2,1,0:T(8,128)(2,1)} %pad_maximum_fusion), calls=%async_computation | async-start | bytes 524288 | tf_op jit(solution)/shard_map/all_to_all | solution.py:29
  7.5 5.8 %all-to-all-done.refs_0_ = bf16[4,128,256]{2,1,0:T(8,128)(2,1)S(1)} async-done(((bf16[4,128,256]{2,1,0:T(8,128)(2,1)}), bf16[4,128,256]{2,1,0:T(8,128)(2,1)S(1)}, u32[]{:S(2)}, u32[]{:S(2)}) %all-to-all-start) | async-done | bytes 262176 | tf_op jit(solution)/shard_map/all_to_all | solution.py:29
  14.9 5.5 %all-to-all-start.1 = ((bf16[16,2,64,512]{3,2,1,0:T(8,128)(2,1)}), bf16[16,2,64,512]{3,2,1,0:T(8,128)(2,1)S(1)}, u32[]{:S(2)}, u32[]{:S(2)}) async-start(bf16[16,2,64,512]{3,2,1,0:T(8,128)(2,1)} %broadcast_in_dim.4), calls=%async_computation.1 | async-start | bytes 4194304 | tf_op jit(solution)/shard_map/all_to_all | solution.py:29
  20.4 5.9 %collective-permute-start = (bf16[4,128,256]{2,1,0:T(8,128)(2,1)S(1)}, bf16[4,128,256]{2,1,0:T(8,128)(2,1)S(1)}, u32[]{:S(2)}, u32[]{:S(2)}) collective-permute-start(bf16[4,128,256]{2,1,0:T(8,128)(2,1)S(1)} %all-to-all-done.refs_0_), channel_id=1, source_target_pairs={{0,56},{8,0},{16,8},{24,16},{32,24},{40,32},{48,40},{56,48},{1,57}... | collective-permute-start | bytes 786440 | tf_op jit(solution)/shard_map/ppermute | solution.py:25
  26.3 3.9 %collective-permute-done.refs_1_ = bf16[4,128,256]{2,1,0:T(8,128)(2,1)S(1)} collective-permute-done((bf16[4,128,256]{2,1,0:T(8,128)(2,1)S(1)}, bf16[4,128,256]{2,1,0:T(8,128)(2,1)S(1)}, u32[]{:S(2)}, u32[]{:S(2)}) %collective-permute-start) | collective-permute-done | bytes 262176 | tf_op jit(solution)/shard_map/ppermute | solution.py:25
  30.1 3.7 %collective-permute-start.1 = (bf16[4,128,256]{2,1,0:T(8,128)(2,1)S(1)}, bf16[4,128,256]{2,1,0:T(8,128)(2,1)S(1)}, u32[]{:S(2)}, u32[]{:S(2)}) collective-permute-start(bf16[4,128,256]{2,1,0:T(8,128)(2,1)S(1)} %collective-permute-done.refs_1_), channel_id=1, source_target_pairs={{0,56},{8,0},{16,8},{24,16},{32,24},{40,32},{48,40},{56,48},{1,57}... | collective-permute-start | bytes 786440 | tf_op jit(solution)/shard_map/ppermute | solution.py:25
  33.8 3.9 %collective-permute-done.1.refs_2_ = bf16[4,128,256]{2,1,0:T(8,128)(2,1)S(1)} collective-permute-done((bf16[4,128,256]{2,1,0:T(8,128)(2,1)S(1)}, bf16[4,128,256]{2,1,0:T(8,128)(2,1)S(1)}, u32[]{:S(2)}, u32[]{:S(2)}) %collective-permute-start.1) | collective-permute-done | bytes 262176 | tf_op jit(solution)/shard_map/ppermute | solution.py:25
  37.7 3.7 %collective-permute-start.2 = (bf16[4,128,256]{2,1,0:T(8,128)(2,1)S(1)}, bf16[4,128,256]{2,1,0:T(8,128)(2,1)S(1)}, u32[]{:S(2)}, u32[]{:S(2)}) collective-permute-start(bf16[4,128,256]{2,1,0:T(8,128)(2,1)S(1)} %collective-permute-done.1.refs_2_), channel_id=1, source_target_pairs={{0,56},{8,0},{16,8},{24,16},{32,24},{40,32},{48,40},{56,48},{1,57}... | collective-permute-start | bytes 786440 | tf_op jit(solution)/shard_map/ppermute | solution.py:25
  45.4 4.0 %collective-permute-done.5.refs_4_ = bf16[4,128,256]{2,1,0:T(8,128)(2,1)S(1)} collective-permute-done((bf16[4,128,256]{2,1,0:T(8,128)(2,1)S(1)}, bf16[4,128,256]{2,1,0:T(8,128)(2,1)S(1)}, u32[]{:S(2)}, u32[]{:S(2)}) %collective-permute-start.5) | collective-permute-done | bytes 262176 | tf_op jit(solution)/shard_map/ppermute | solution.py:25
  50.9 3.7 %collective-permute-start.8 = (bf16[2,128,256]{2,1,0:T(8,128)(2,1)}, bf16[2,128,256]{2,1,0:T(8,128)(2,1)}, u32[]{:S(2)}, u32[]{:S(2)}) collective-permute-start(bf16[2,128,256]{2,1,0:T(8,128)(2,1)} %slice.142), channel_id=1, source_target_pairs={{0,56},{8,0},{16,8},{24,16},{32,24},{40,32},{48,40},{56,48},{1,57}... | collective-permute-start | bytes 393224 | tf_op jit(solution)/shard_map/ppermute | solution.py:25
  58.9 5.9 %views.1 = (bf16[4,512,256]{2,1,0:T(8,128)(2,1)}, bf16[4,512,256]{2,1,0:T(8,128)(2,1)}, f32[2,256,256]{2,1,0:T(8,128)}, bf16[272,256]{1,0:T(8,128)(2,1)}, bf16[272,256]{1,0:T(8,128)(2,1)}, /*index=5*/f32[8,256]{1,0:T(8,128)}) custom-call(s32[2]{0:T(128)} %pad_add_fusion.place_ref, bf16[4,4,2,64,512]{4,3,2,1,0:T(8,128)(2,1)} %bitcast.97, ...), custom_call_target="tpu_custom_call" | custom-call | tf_op jit(solution)/shard_map/views/pallas_call | solution.py:251
  100.3 4.1 %gram.1 = (bf16[2048,512]{1,0:T(8,128)(2,1)}, bf16[256,2176]{1,0:T(8,128)(2,1)}, f32[8,512]{1,0:T(8,128)}) custom-call(f32[1,1]{1,0:T(1,128)} %bitcast.11.diff_ref, bf16[144,512]{1,0:T(8,128)(2,1)} %copy-done.5, bf16[128,512]{1,0:T(8,128)(2,1)} %copy-done.8, bf16[144,512]{1,0:T(8,128)(2,1)} %copy-done.15, bf16[128,512]{1,0:T(8,128)(2,1)} %copy-done.21, ...), custom_call_target="tpu_custom_call" | custom-call | tf_op jit(solution)/shard_map/gram/pallas_call | solution.py:290
  104.4 6.7 %all-to-all-start.2 = ((bf16[16,16,2176]{2,1,0:T(8,128)(2,1)}), bf16[16,16,2176]{2,1,0:T(8,128)(2,1)S(1)}, u32[]{:S(2)}, u32[]{:S(2)}) async-start(bf16[16,16,2176]{2,1,0:T(8,128)(2,1)} %bitcast.106), calls=%async_computation.2 | async-start | bytes 2228224 | tf_op jit(solution)/shard_map/all_to_all | solution.py:29
  113.9 11.3 %all-to-all-done.2 = bf16[16,16,2176]{2,1,0:T(8,128)(2,1)S(1)} async-done(((bf16[16,16,2176]{2,1,0:T(8,128)(2,1)}), bf16[16,16,2176]{2,1,0:T(8,128)(2,1)S(1)}, u32[]{:S(2)}, u32[]{:S(2)}) %all-to-all-start.2) | async-done | bytes 1114144 | tf_op jit(solution)/shard_map/all_to_all | solution.py:29
  126.2 18.7 %all_to_all.30 = bf16[16,16,2048]{2,1,0:T(8,128)(2,1)S(1)} all-to-all(bf16[16,16,2048]{2,1,0:T(8,128)(2,1)S(1)} %broadcast_in_dim.5), channel_id=1, replica_groups=mesh['x'=4,'z'=8,'y'=4,'c'=2] {'x','y'}, dimensions={0} | all-to-all | bytes 2097152 | tf_op jit(solution)/shard_map/all_to_all | solution.py:29
  150.4 4.4 %far_terms.1 = (bf16[256,256]{1,0:T(8,128)(2,1)}, bf16[272,256]{1,0:T(8,128)(2,1)}) custom-call(s32[2]{0:T(128)} %pad_add_fusion.place_ref, bf16[4,4,2,64,512]{4,3,2,1,0:T(8,128)(2,1)} %bitcast.98, bf16[4,4,2,64,512]{4,3,2,1,0:T(8,128)(2,1)} %collective-permute-done.6.oth_ref, bf16[512,256]{1,0:T(8,128)(2,1)} %bitcast.102, f32[1,1]{1,0:T(1,128)} %bitcast.22.share_ref), custom_call_target="tpu_custom_call" | custom-call | tf_op jit(solution)/shard_map/far_terms/pallas_call | solution.py:344
  155.5 4.8 %input_terms.1 = bf16[4,512,512]{2,1,0:T(8,128)(2,1)} custom-call(bf16[512,256]{1,0:T(8,128)(2,1)} %bitcast.103, bf16[512,256]{1,0:T(8,128)(2,1)} %copy-done.13, bf16[4,512,256]{2,1,0:T(8,128)(2,1)} %get-tuple-element.50.kept_ref, bf16[4,512,256]{2,1,0:T(8,128)(2,1)} %copy-done.4), custom_call_target="tpu_custom_call" | custom-call | tf_op jit(solution)/shard_map/input_terms/pallas_call | solution.py:359
  160.3 5.1 %all-to-all-start.4 = ((bf16[16,2,64,512]{3,2,1,0:T(8,128)(2,1)}), bf16[16,2,64,512]{3,2,1,0:T(8,128)(2,1)S(1)}, u32[]{:S(2)}, u32[]{:S(2)}) async-start(bf16[16,2,64,512]{3,2,1,0:T(8,128)(2,1)} %bitcast.100), calls=%async_computation.4 | async-start | bytes 4194304 | tf_op jit(solution)/shard_map/all_to_all | solution.py:29
  167.6 4.7 %collective-permute-done.28 = bf16[256,256]{1,0:T(8,128)(2,1)S(1)} collective-permute-done((bf16[256,256]{1,0:T(8,128)(2,1)S(1)}, bf16[256,256]{1,0:T(8,128)(2,1)S(1)}, u32[]{:S(2)}, u32[]{:S(2)}) %collective-permute-start.28) | collective-permute-done | bytes 131104 | tf_op jit(solution)/shard_map/ppermute | solution.py:25
  172.2 5.5 %weight_terms.1 = bf16[8,528,256]{2,1,0:T(8,128)(2,1)} custom-call(s32[2]{0:T(128)} %pad_add_fusion.place_ref, bf16[4,4,2,64,512]{4,3,2,1,0:T(8,128)(2,1)} %bitcast.99, bf16[4,4,2,64,512]{4,3,2,1,0:T(8,128)(2,1)} %collective-permute-done.6.oth_ref, bf16[512,256]{1,0:T(8,128)(2,1)} %bitcast.104, f32[1,1]{1,0:T(1,128)} %bitcast.22.share_ref), custom_call_target="tpu_custom_call" | custom-call | tf_op jit(solution)/shard_map/weight_terms/pallas_call | solution.py:371
  182.2 5.6 %collective-permute-done.30 = bf16[528,256]{1,0:T(8,128)(2,1)S(1)} collective-permute-done((bf16[528,256]{1,0:T(8,128)(2,1)S(1)}, bf16[528,256]{1,0:T(8,128)(2,1)S(1)}, u32[]{:S(2)}, u32[]{:S(2)}) %collective-permute-start.30) | collective-permute-done | bytes 270368 | tf_op jit(solution)/shard_map/ppermute | solution.py:25
  192.3 4.7 %collective-permute-done.32 = bf16[528,256]{1,0:T(8,128)(2,1)S(1)} collective-permute-done((bf16[528,256]{1,0:T(8,128)(2,1)S(1)}, bf16[528,256]{1,0:T(8,128)(2,1)S(1)}, u32[]{:S(2)}, u32[]{:S(2)}) %collective-permute-start.32) | collective-permute-done | bytes 270368 | tf_op jit(solution)/shard_map/ppermute | solution.py:25
  201.5 4.4 %collective-permute-done.34 = bf16[528,256]{1,0:T(8,128)(2,1)S(1)} collective-permute-done((bf16[528,256]{1,0:T(8,128)(2,1)S(1)}, bf16[528,256]{1,0:T(8,128)(2,1)S(1)}, u32[]{:S(2)}, u32[]{:S(2)}) %collective-permute-start.34) | collective-permute-done | bytes 270368 | tf_op jit(solution)/shard_map/ppermute | solution.py:25
  207.7 4.3 %all-to-all-start.5 = ((bf16[4,128,256]{2,1,0:T(8,128)(2,1)}), bf16[4,128,256]{2,1,0:T(8,128)(2,1)S(1)}, u32[]{:S(2)}, u32[]{:S(2)}) async-start(bf16[4,128,256]{2,1,0:T(8,128)(2,1)} %bitcast.30), calls=%async_computation.5 | async-start | bytes 524288 | tf_op jit(solution)/shard_map/all_to_all | solution.py:29
  (171 shorter events, 80.4 us)
Async XLA Ops:
  2.3 11.0 %all-to-all-start = ((bf16[4,128,256]{2,1,0:T(8,128)(2,1)}), bf16[4,128,256]{2,1,0:T(8,128)(2,1)S(1)}, u32[]{:S(2)}, u32[]{:S(2)}) async-start(bf16[4,128,256]{2,1,0:T(8,128)(2,1)} %pad_maximum_fusion), calls=%async_computation | async-start | bytes 524288 | tf_op jit(solution)/shard_map/all_to_all | solution.py:29
  14.9 34.5 %all-to-all-start.1 = ((bf16[16,2,64,512]{3,2,1,0:T(8,128)(2,1)}), bf16[16,2,64,512]{3,2,1,0:T(8,128)(2,1)S(1)}, u32[]{:S(2)}, u32[]{:S(2)}) async-start(bf16[16,2,64,512]{3,2,1,0:T(8,128)(2,1)} %broadcast_in_dim.4), calls=%async_computation.1 | async-start | bytes 4194304 | tf_op jit(solution)/shard_map/all_to_all | solution.py:29
  20.4 9.7 %collective-permute-start = (bf16[4,128,256]{2,1,0:T(8,128)(2,1)S(1)}, bf16[4,128,256]{2,1,0:T(8,128)(2,1)S(1)}, u32[]{:S(2)}, u32[]{:S(2)}) collective-permute-start(bf16[4,128,256]{2,1,0:T(8,128)(2,1)S(1)} %all-to-all-done.refs_0_), channel_id=1, source_target_pairs={{0,56},{8,0},{16,8},{24,16},{32,24},{40,32},{48,40},{56,48},{1,57}... | collective-permute-start | bytes 786440 | tf_op jit(solution)/shard_map/ppermute | solution.py:25
  33.8 7.9 %collective-permute-start.4 = (bf16[4,128,256]{2,1,0:T(8,128)(2,1)S(1)}, bf16[4,128,256]{2,1,0:T(8,128)(2,1)S(1)}, u32[]{:S(2)}, u32[]{:S(2)}) collective-permute-start(bf16[4,128,256]{2,1,0:T(8,128)(2,1)S(1)} %collective-permute-done.3.refs_6_), channel_id=1, source_target_pairs={{0,8},{8,16},{16,24},{24,32},{32,40},{40,48},{48,56},{56,0},{1,9},... | collective-permute-start | bytes 786440 | tf_op jit(solution)/shard_map/ppermute | solution.py:25
  49.3 8.9 %collective-permute-start.6 = (bf16[4,4,2,64,512]{4,3,2,1,0:T(8,128)(2,1)S(1)}, bf16[4,4,2,64,512]{4,3,2,1,0:T(8,128)(2,1)}, u32[]{:S(2)}, u32[]{:S(2)}) collective-permute-start(bf16[4,4,2,64,512]{4,3,2,1,0:T(8,128)(2,1)S(1)} %bitcast.96), channel_id=1, source_target_pairs={{0,1},{1,0},{2,3},{3,2},{4,5},{5,4},{6,7},{7,6},{8,9},{9,8},{10,11... | collective-permute-start | bytes 6291464 | tf_op jit(solution)/shard_map/ppermute | solution.py:21
  50.2 8.0 %collective-permute-start.7 = (bf16[2,128,256]{2,1,0:T(8,128)(2,1)}, bf16[2,128,256]{2,1,0:T(8,128)(2,1)S(1)}, u32[]{:S(2)}, u32[]{:S(2)}) collective-permute-start(bf16[2,128,256]{2,1,0:T(8,128)(2,1)} %slice.141), channel_id=1, source_target_pairs={{0,8},{8,16},{16,24},{24,32},{32,40},{40,48},{48,56},{56,0},{1,9},... | collective-permute-start | bytes 393224 | tf_op jit(solution)/shard_map/ppermute | solution.py:25
  66.6 9.3 %collective-permute-start.11 = (bf16[128,512]{1,0:T(8,128)(2,1)S(1)}, bf16[128,512]{1,0:T(8,128)(2,1)S(1)}, u32[]{:S(2)}, u32[]{:S(2)}) collective-permute-start(bf16[128,512]{1,0:T(8,128)(2,1)S(1)} %slice.144.refs_1_), channel_id=1, source_target_pairs={{0,56},{8,0},{16,8},{24,16},{32,24},{40,32},{48,40},{56,48},{1,57}... | collective-permute-start | bytes 393224 | tf_op jit(solution)/shard_map/ppermute | solution.py:25
  73.9 7.9 %collective-permute-start.17 = (bf16[144,512]{1,0:T(8,128)(2,1)S(1)}, bf16[144,512]{1,0:T(8,128)(2,1)S(1)}, u32[]{:S(2)}, u32[]{:S(2)}) collective-permute-start(bf16[144,512]{1,0:T(8,128)(2,1)S(1)} %collective-permute-done.16.refs_14_), channel_id=1, source_target_pairs={{0,8},{8,16},{16,24},{24,32},{32,40},{40,48},{48,56},{56,0},{1,9},... | collective-permute-start | bytes 442376 | tf_op jit(solution)/shard_map/ppermute | solution.py:25
  73.9 9.6 %collective-permute-start.21 = (bf16[128,512]{1,0:T(8,128)(2,1)S(1)}, bf16[128,512]{1,0:T(8,128)(2,1)S(1)}, u32[]{:S(2)}, u32[]{:S(2)}) collective-permute-start(bf16[128,512]{1,0:T(8,128)(2,1)S(1)} %slice.144.refs_1_), channel_id=1, source_target_pairs={{0,8},{8,16},{16,24},{24,32},{32,40},{40,48},{48,56},{56,0},{1,9},... | collective-permute-start | bytes 393224 | tf_op jit(solution)/shard_map/ppermute | solution.py:25
  77.5 12.5 %collective-permute-start.12 = (bf16[144,512]{1,0:T(8,128)(2,1)S(1)}, bf16[144,512]{1,0:T(8,128)(2,1)S(1)}, u32[]{:S(2)}, u32[]{:S(2)}) collective-permute-start(bf16[144,512]{1,0:T(8,128)(2,1)S(1)} %collective-permute-done.10.refs_2_), channel_id=1, source_target_pairs={{0,56},{8,0},{16,8},{24,16},{32,24},{40,32},{48,40},{56,48},{1,57}... | collective-permute-start | bytes 442376 | tf_op jit(solution)/shard_map/ppermute | solution.py:25
  81.8 11.6 %collective-permute-start.18 = (bf16[144,512]{1,0:T(8,128)(2,1)S(1)}, bf16[144,512]{1,0:T(8,128)(2,1)S(1)}, u32[]{:S(2)}, u32[]{:S(2)}) collective-permute-start(bf16[144,512]{1,0:T(8,128)(2,1)S(1)} %collective-permute-done.17.refs_12_), channel_id=1, source_target_pairs={{0,8},{8,16},{16,24},{24,32},{32,40},{40,48},{48,56},{56,0},{1,9},... | collective-permute-start | bytes 442376 | tf_op jit(solution)/shard_map/ppermute | solution.py:25
  83.5 9.7 %collective-permute-start.15 = (bf16[128,512]{1,0:T(8,128)(2,1)S(1)}, bf16[128,512]{1,0:T(8,128)(2,1)S(1)}, u32[]{:S(2)}, u32[]{:S(2)}) collective-permute-start(bf16[128,512]{1,0:T(8,128)(2,1)S(1)} %collective-permute-done.13.refs_5_), channel_id=1, source_target_pairs={{0,56},{8,0},{16,8},{24,16},{32,24},{40,32},{48,40},{56,48},{1,57}... | collective-permute-start | bytes 393224 | tf_op jit(solution)/shard_map/ppermute | solution.py:25
  90.0 8.4 %collective-permute-start.23 = (bf16[128,512]{1,0:T(8,128)(2,1)S(1)}, bf16[128,512]{1,0:T(8,128)(2,1)S(1)}, u32[]{:S(2)}, u32[]{:S(2)}) collective-permute-start(bf16[128,512]{1,0:T(8,128)(2,1)S(1)} %collective-permute-done.22.refs_13_), channel_id=1, source_target_pairs={{0,8},{8,16},{16,24},{24,32},{32,40},{40,48},{48,56},{56,0},{1,9},... | collective-permute-start | bytes 393224 | tf_op jit(solution)/shard_map/ppermute | solution.py:25
  90.0 8.4 %collective-permute-start.14 = (bf16[144,512]{1,0:T(8,128)(2,1)S(1)}, bf16[144,512]{1,0:T(8,128)(2,1)S(1)}, u32[]{:S(2)}, u32[]{:S(2)}) collective-permute-start(bf16[144,512]{1,0:T(8,128)(2,1)S(1)} %collective-permute-done.12.refs_4_), channel_id=1, source_target_pairs={{0,56},{8,0},{16,8},{24,16},{32,24},{40,32},{48,40},{56,48},{1,57}... | collective-permute-start | bytes 442376 | tf_op jit(solution)/shard_map/ppermute | solution.py:25
  104.4 20.8 %all-to-all-start.2 = ((bf16[16,16,2176]{2,1,0:T(8,128)(2,1)}), bf16[16,16,2176]{2,1,0:T(8,128)(2,1)S(1)}, u32[]{:S(2)}, u32[]{:S(2)}) async-start(bf16[16,16,2176]{2,1,0:T(8,128)(2,1)} %bitcast.106), calls=%async_computation.2 | async-start | bytes 2228224 | tf_op jit(solution)/shard_map/all_to_all | solution.py:29
  111.1 14.9 %collective-permute-start.25 = (bf16[4,512,256]{2,1,0:T(8,128)(2,1)S(1)}, bf16[4,512,256]{2,1,0:T(8,128)(2,1)S(1)}, u32[]{:S(2)}, u32[]{:S(2)}) collective-permute-start(bf16[4,512,256]{2,1,0:T(8,128)(2,1)S(1)} %copy-done.31), channel_id=1, source_target_pairs={{0,1},{1,0},{2,3},{3,2},{4,5},{5,4},{6,7},{7,6},{8,9},{9,8},{10,11... | collective-permute-start | bytes 3145736 | tf_op jit(solution)/shard_map/ppermute | solution.py:21
  154.8 17.5 %collective-permute-start.29 = (bf16[272,256]{1,0:T(8,128)(2,1)}, bf16[272,256]{1,0:T(8,128)(2,1)S(1)}, u32[]{:S(2)}, u32[]{:S(2)}) collective-permute-start(bf16[272,256]{1,0:T(8,128)(2,1)} %get-tuple-element.48), channel_id=1, source_target_pairs={{0,56},{8,0},{16,8},{24,16},{32,24},{40,32},{48,40},{56,48},{1,57}... | collective-permute-start | bytes 417800 | tf_op jit(solution)/shard_map/ppermute | solution.py:25
  160.3 47.4 %all-to-all-start.4 = ((bf16[16,2,64,512]{3,2,1,0:T(8,128)(2,1)}), bf16[16,2,64,512]{3,2,1,0:T(8,128)(2,1)S(1)}, u32[]{:S(2)}, u32[]{:S(2)}) async-start(bf16[16,2,64,512]{3,2,1,0:T(8,128)(2,1)} %bitcast.100), calls=%async_computation.4 | async-start | bytes 4194304 | tf_op jit(solution)/shard_map/all_to_all | solution.py:29
  178.9 8.9 %collective-permute-start.30 = (bf16[528,256]{1,0:T(8,128)(2,1)S(1)}, bf16[528,256]{1,0:T(8,128)(2,1)S(1)}, u32[]{:S(2)}, u32[]{:S(2)}) collective-permute-start(bf16[528,256]{1,0:T(8,128)(2,1)S(1)} %get-tuple-element.71), channel_id=1, source_target_pairs={{0,8},{8,16},{16,24},{24,32},{32,40},{40,48},{48,56},{56,0},{1,9},... | collective-permute-start | bytes 811016 | tf_op jit(solution)/shard_map/ppermute | solution.py:25
  179.5 8.3 %collective-permute-start.31 = (bf16[528,256]{1,0:T(8,128)(2,1)S(1)}, bf16[528,256]{1,0:T(8,128)(2,1)S(1)}, u32[]{:S(2)}, u32[]{:S(2)}) collective-permute-start(bf16[528,256]{1,0:T(8,128)(2,1)S(1)} %get-tuple-element.70), channel_id=1, source_target_pairs={{0,56},{8,0},{16,8},{24,16},{32,24},{40,32},{48,40},{56,48},{1,57}... | collective-permute-start | bytes 811016 | tf_op jit(solution)/shard_map/ppermute | solution.py:25
  189.0 8.0 %collective-permute-start.32 = (bf16[528,256]{1,0:T(8,128)(2,1)S(1)}, bf16[528,256]{1,0:T(8,128)(2,1)S(1)}, u32[]{:S(2)}, u32[]{:S(2)}) collective-permute-start(bf16[528,256]{1,0:T(8,128)(2,1)S(1)} %get-tuple-element.69), channel_id=1, source_target_pairs={{0,8},{8,16},{16,24},{24,32},{32,40},{40,48},{48,56},{56,0},{1,9},... | collective-permute-start | bytes 811016 | tf_op jit(solution)/shard_map/ppermute | solution.py:25
  189.1 8.0 %collective-permute-start.33 = (bf16[528,256]{1,0:T(8,128)(2,1)S(1)}, bf16[528,256]{1,0:T(8,128)(2,1)S(1)}, u32[]{:S(2)}, u32[]{:S(2)}) collective-permute-start(bf16[528,256]{1,0:T(8,128)(2,1)S(1)} %get-tuple-element.68), channel_id=1, source_target_pairs={{0,56},{8,0},{16,8},{24,16},{32,24},{40,32},{48,40},{56,48},{1,57}... | collective-permute-start | bytes 811016 | tf_op jit(solution)/shard_map/ppermute | solution.py:25
  198.2 7.7 %collective-permute-start.34 = (bf16[528,256]{1,0:T(8,128)(2,1)S(1)}, bf16[528,256]{1,0:T(8,128)(2,1)S(1)}, u32[]{:S(2)}, u32[]{:S(2)}) collective-permute-start(bf16[528,256]{1,0:T(8,128)(2,1)S(1)} %get-tuple-element.66), channel_id=1, source_target_pairs={{0,8},{8,16},{16,24},{24,32},{32,40},{40,48},{48,56},{56,0},{1,9},... | collective-permute-start | bytes 811016 | tf_op jit(solution)/shard_map/ppermute | solution.py:25
  207.7 10.9 %all-to-all-start.5 = ((bf16[4,128,256]{2,1,0:T(8,128)(2,1)}), bf16[4,128,256]{2,1,0:T(8,128)(2,1)S(1)}, u32[]{:S(2)}, u32[]{:S(2)}) async-start(bf16[4,128,256]{2,1,0:T(8,128)(2,1)} %bitcast.30), calls=%async_computation.5 | async-start | bytes 524288 | tf_op jit(solution)/shard_map/all_to_all | solution.py:29
  (51 other events, 519.3 us)
where the time goes:
time: 222 us; the launch traced here: 221 us
  starting transfers between devices  75.9 us (34%)
  waiting for transfers between devices  73.4 us (33%)
  Pallas kernels  24.7 us (11%)
  blocking collectives  18.7 us (8%)
  other arithmetic  13.1 us (6%)
  local copies, waits for them, and re-layouts  8.56 us (4%)
  between operations  5.57 us (3%)
    ppermute x30, starting transfers between devices, hop(): return lax.ppermute(v, 'z', [(i, (i + k) % NZ) for i in range(NZ)])  48.7 us
    ppermute x30, waiting for transfers between devices, hop(): return lax.ppermute(v, 'z', [(i, (i + k) % NZ) for i in range(NZ)])  48.4 us
    all_to_all x5, starting transfers between devices, exchange(): return lax.all_to_all(v, axes, split_axis=0, concat_axis=0, tiled=True)  25.9 us
    all_to_all x5, waiting for transfers between devices, exchange(): return lax.all_to_all(v, axes, split_axis=0, concat_axis=0, tiled=True)  20.6 us
    all_to_all x1, blocking collectives, exchange(): return lax.all_to_all(v, axes, split_axis=0, concat_axis=0, tiled=True)  18.7 us
    pallas_call x1, Pallas kernels, on_device(): pl.pallas_call(views_kernel, grid=(NY,), in_specs=[smem, at_dim(hblock, 1...  5.9 us
    pallas_call x1, Pallas kernels, on_device(): pl.pallas_call(weight_kernel, grid=(NY,), in_specs=[smem, at_dim(hblock,...  5.51 us
    pallas_call x1, Pallas kernels, on_device(): pl.pallas_call(input_kernel, grid=(NY,), in_specs=[fixed((flat, sub)), fi...  4.83 us
  transfers between devices with their start and end apart: 42, of which 22 were waited for; matrix products, arithmetic and copies ran while one was open for 7% of the time, Pallas kernels for 7%

commit v1 on v0

--- a/solution.py
+++ b/solution.py
@@ -172,14 +172,22 @@
     return out
 
 
+def turn_kernel(own_ref, oth_ref, kept_ref, recv_ref, own_out, oth_out, w_out):
+    own_out[0] = flat_rows(own_ref).T
+    oth_out[0] = flat_rows(oth_ref).T
+    sub = kept_ref.shape[2]
+    w_out[0, :sub] = kept_ref[0].T
+    w_out[0, sub:] = recv_ref[0].T
+
+
 def weight_kernel(place_ref, own_ref, oth_ref, g_ref, share_ref, out_ref):
     step = pl.program_id(0)
     core = place_ref[0]
     zi = place_ref[1]
-    rows = NY * (own_ref.shape[4] // HALF)
-    kz = rows // NY
+    kz = own_ref.shape[1] // HALF
+    rows = NY * kz
     for ref, lead in ((own_ref, core), (oth_ref, 1 - core)):
-        term = dot(flat_rows(ref), g_ref[...], 0, 0).astype(BF)
+        term = dot(ref[0], g_ref[...], 1, 0).astype(BF)
         for q in range(HALF):
             k = lax.rem(lead * HALF + q - zi + NZ, NZ)
             out_ref[k, pl.ds(pl.multiple_of(step * kz, kz), kz)] = term[q * kz : (q + 1) * kz]
@@ -197,10 +205,10 @@
     step = pl.program_id(0)
     core = place_ref[0]
     zi = place_ref[1]
-    kz = own_ref.shape[4]
+    kz = own_ref.shape[1]
     mine = 1 - zi // HALF == core
-    block = jnp.where(mine, flat_rows(own_ref).astype(F32), flat_rows(oth_ref).astype(F32)).astype(BF)
-    term = dot(block, g_ref[...], 0, 0).astype(BF)
+    block = jnp.where(mine, own_ref[0].astype(F32), oth_ref[0].astype(F32)).astype(BF)
+    term = dot(block, g_ref[...], 1, 0).astype(BF)
     place = pl.ds(pl.multiple_of(lax.rem(step, NY // 2) * kz, kz), kz)
 
     @pl.when(step < NY // 2)
@@ -218,8 +226,9 @@
         b_ref[NY // 2 * kz :] = in_lanes(share_ref[...], lane, 3 * zi, row == 0).astype(BF)
 
 
-def input_kernel(own_ref, oth_ref, kept_ref, recv_ref, out_ref):
-    term = dot(own_ref[...], kept_ref[0], 1, 1) + dot(oth_ref[...], recv_ref[0], 1, 1)
+def input_kernel(own_ref, oth_ref, w_ref, out_ref):
+    sub = own_ref.shape[1]
+    term = dot(own_ref[...], w_ref[0, :sub], 1, 0) + dot(oth_ref[...], w_ref[0, sub:], 1, 0)
     out_ref[0] = term.astype(BF)
 
 
@@ -309,9 +318,20 @@
     deviation = jnp.sqrt(variance + 0.0001)
 
     pieces = exchange(gram_part.reshape(NX * NY, blk // (NX * NY), wide), CHIPS)
+    turned = (NY, kpart, flat)
+    h_own, h_oth, w_turned = pl.pallas_call(
+        turn_kernel,
+        grid=(NY,),
+        in_specs=[at_dim(hblock, 1), at_dim(hblock, 1)] + [at_dim((1, kpart, sub), 0)] * 2,
+        out_specs=[at_dim((1, kpart, flat), 0)] * 2 + [at_dim((1, 2 * sub, kpart), 0)],
+        out_shape=[shape(turned, BF), shape(turned, BF), shape((NY, 2 * sub, kpart), BF)],
+        name="turn",
+    )(h_own, h_oth, w_kept, w_recv)
     gram_rows = jnp.sum(pieces[:, :, : NZ * blk].astype(F32), axis=0).astype(BF)
     share = jnp.sum(pieces[:, :, NZ * blk :].astype(F32))
-    gram_rows, share, variance, w_recv = lax.optimization_barrier((gram_rows, share, variance, w_recv))
+    gram_rows, share, variance, h_own, h_oth, w_turned = lax.optimization_barrier(
+        (gram_rows, share, variance, h_own, h_oth, w_turned)
+    )
     gram_half = exchange(copies(gram_rows, NX * NY), CHIPS).reshape(blk, NZ * blk)
     squares = gram_half.astype(F32)
     share = (share + jnp.sum(squares * squares) / ((total_rows - 1.0) ** 2 * full_width)).reshape(1, 1)
@@ -338,7 +358,7 @@
     grad_views = (inv_grad + hinge_grad + cov_grad).astype(BF)
     grads = grad_views.reshape(2, NX, rows, sub).transpose(1, 0, 2, 3).reshape(flat, sub)
 
-    far_block = pl.BlockSpec((NX, 1, 2, rows, kz), lambda j, place: (0, j, 0, 0, lax.rem(place[1], HALF)))
+    far_block = pl.BlockSpec((1, kz, flat), lambda j, place: (j, lax.rem(place[1], HALF), 0))
     held = lambda s: pl.BlockSpec(s, lambda j, place: (0,) * len(s))
     half = NX // 2 * kz
     far_right, far_left = pl.pallas_call(
@@ -359,11 +379,11 @@
     input_part = pl.pallas_call(
         input_kernel,
         grid=(NY,),
-        in_specs=[fixed((flat, sub)), fixed((flat, sub)), at_dim((1, kpart, sub), 0), at_dim((1, kpart, sub), 0)],
+        in_specs=[fixed((flat, sub)), fixed((flat, sub)), at_dim((1, 2 * sub, kpart), 0)],
         out_specs=at_dim((1, flat, kpart), 0),
         out_shape=shape((NY, flat, kpart), BF),
         name="input_terms",
-    )(later, swap_core(grads), w_kept, w_recv)
+    )(later, swap_core(grads), w_turned)
     input_parts = exchange(input_part.reshape(NX * NY, 2, rows, kpart), ("y", "x"))
 
     later, _ = lax.optimization_barrier((later, input_part))
@@ -371,7 +391,7 @@
     weight_part = pl.pallas_call(
         weight_kernel,
         grid=(NY,),
-        in_specs=[smem, at_dim(hblock, 1), at_dim(hblock, 1), fixed((flat, sub)), fixed((1, 1))],
+        in_specs=[smem] + [at_dim((1, kpart, flat), 0)] * 2 + [fixed((flat, sub)), fixed((1, 1))],
         out_specs=fixed((NZ, terms, sub)),
         out_shape=shape((NZ, terms, sub), BF),
         name="weight_terms",

time: 222 us -> 221 us (level)
  waiting for transfers between devices: 73.4 us -> 66.8 us
  Pallas kernels: 24.7 us -> 30 us
    pallas_call x1 -> x2, Pallas kernels: 5.51 us -> 11.3 us  [the longest x1 5.87 us: on_device(): pl.pallas_call(turn_kernel, grid=(NY,), in_specs=[at_dim(hblock, 1), at_d...]
    all_to_all x5, waiting for transfers between devices: 20.6 us -> 15.1 us  [exchange(): return lax.all_to_all(v, axes, split_axis=0, concat_axis=0, tiled=True)]
  transfers between devices with their start and end apart: 42 -> 42, of which waited for: 22 -> 22; matrix products, arithmetic and copies ran while one was open for 7% -> 7% of each run, Pallas kernels for 7% -> 11%
where the time goes in v1:
time: 221 us; the launch traced here: 220 us
  starting transfers between devices  75.4 us (34%)
  waiting for transfers between devices  66.8 us (30%)
  Pallas kernels  30 us (14%)
  blocking collectives  18.6 us (8%)
  other arithmetic  13.1 us (6%)
  local copies, waits for them, and re-layouts  9.62 us (4%)
  between operations  5.55 us (3%)
    ppermute x30, starting transfers between devices, hop(): return lax.ppermute(v, 'z', [(i, (i + k) % NZ) for i in range(NZ)])  48.7 us
    ppermute x30, waiting for transfers between devices, hop(): return lax.ppermute(v, 'z', [(i, (i + k) % NZ) for i in range(NZ)])  48.3 us
    all_to_all x5, starting transfers between devices, exchange(): return lax.all_to_all(v, axes, split_axis=0, concat_axis=0, tiled=True)  25.9 us
    all_to_all x1, blocking collectives, exchange(): return lax.all_to_all(v, axes, split_axis=0, concat_axis=0, tiled=True)  18.6 us
    all_to_all x5, waiting for transfers between devices, exchange(): return lax.all_to_all(v, axes, split_axis=0, concat_axis=0, tiled=True)  15.1 us
    pallas_call x1, Pallas kernels, on_device(): pl.pallas_call(views_kernel, grid=(NY,), in_specs=[smem, at_dim(hblock, 1...  5.98 us
    pallas_call x1, Pallas kernels, on_device(): pl.pallas_call(turn_kernel, grid=(NY,), in_specs=[at_dim(hblock, 1), at_d...  5.87 us
    pallas_call x1, Pallas kernels, on_device(): pl.pallas_call(weight_kernel, grid=(NY,), in_specs=[smem] + [at_dim((1, k...  5.39 us
  transfers between devices with their start and end apart: 42, of which 22 were waited for; matrix products, arithmetic and copies ran while one was open for 7% of the time, Pallas kernels for 11%

profile of v1, /device:TPU:8, one launch (start us, length us, event | category | flops | bytes accessed | tf_op | source)
XLA Modules:
  0.0 219.8 jit_solution(12098800257695763828)
XLA Ops:
  2.3 4.3 %all-to-all-start = ((bf16[4,128,256]{2,1,0:T(8,128)(2,1)}), bf16[4,128,256]{2,1,0:T(8,128)(2,1)S(1)}, u32[]{:S(2)}, u32[]{:S(2)}) async-start(bf16[4,128,256]{2,1,0:T(8,128)(2,1)} %pad_maximum_fusion), calls=%async_computation | async-start | bytes 524288 | tf_op jit(solution)/shard_map/all_to_all | solution.py:29
  7.5 5.8 %all-to-all-done.refs_0_ = bf16[4,128,256]{2,1,0:T(8,128)(2,1)S(1)} async-done(((bf16[4,128,256]{2,1,0:T(8,128)(2,1)}), bf16[4,128,256]{2,1,0:T(8,128)(2,1)S(1)}, u32[]{:S(2)}, u32[]{:S(2)}) %all-to-all-start) | async-done | bytes 262176 | tf_op jit(solution)/shard_map/all_to_all | solution.py:29
  14.9 5.5 %all-to-all-start.1 = ((bf16[16,2,64,512]{3,2,1,0:T(8,128)(2,1)}), bf16[16,2,64,512]{3,2,1,0:T(8,128)(2,1)S(1)}, u32[]{:S(2)}, u32[]{:S(2)}) async-start(bf16[16,2,64,512]{3,2,1,0:T(8,128)(2,1)} %broadcast_in_dim.4), calls=%async_computation.1 | async-start | bytes 4194304 | tf_op jit(solution)/shard_map/all_to_all | solution.py:29
  20.4 5.9 %collective-permute-start = (bf16[4,128,256]{2,1,0:T(8,128)(2,1)S(1)}, bf16[4,128,256]{2,1,0:T(8,128)(2,1)S(1)}, u32[]{:S(2)}, u32[]{:S(2)}) collective-permute-start(bf16[4,128,256]{2,1,0:T(8,128)(2,1)S(1)} %all-to-all-done.refs_0_), channel_id=1, source_target_pairs={{0,56},{8,0},{16,8},{24,16},{32,24},{40,32},{48,40},{56,48},{1,57}... | collective-permute-start | bytes 786440 | tf_op jit(solution)/shard_map/ppermute | solution.py:25
  26.3 3.9 %collective-permute-done.refs_1_ = bf16[4,128,256]{2,1,0:T(8,128)(2,1)S(1)} collective-permute-done((bf16[4,128,256]{2,1,0:T(8,128)(2,1)S(1)}, bf16[4,128,256]{2,1,0:T(8,128)(2,1)S(1)}, u32[]{:S(2)}, u32[]{:S(2)}) %collective-permute-start) | collective-permute-done | bytes 262176 | tf_op jit(solution)/shard_map/ppermute | solution.py:25
  30.1 3.7 %collective-permute-start.1 = (bf16[4,128,256]{2,1,0:T(8,128)(2,1)S(1)}, bf16[4,128,256]{2,1,0:T(8,128)(2,1)S(1)}, u32[]{:S(2)}, u32[]{:S(2)}) collective-permute-start(bf16[4,128,256]{2,1,0:T(8,128)(2,1)S(1)} %collective-permute-done.refs_1_), channel_id=1, source_target_pairs={{0,56},{8,0},{16,8},{24,16},{32,24},{40,32},{48,40},{56,48},{1,57}... | collective-permute-start | bytes 786440 | tf_op jit(solution)/shard_map/ppermute | solution.py:25
  33.8 3.9 %collective-permute-done.1.refs_2_ = bf16[4,128,256]{2,1,0:T(8,128)(2,1)S(1)} collective-permute-done((bf16[4,128,256]{2,1,0:T(8,128)(2,1)S(1)}, bf16[4,128,256]{2,1,0:T(8,128)(2,1)S(1)}, u32[]{:S(2)}, u32[]{:S(2)}) %collective-permute-start.1) | collective-permute-done | bytes 262176 | tf_op jit(solution)/shard_map/ppermute | solution.py:25
  37.7 3.7 %collective-permute-start.2 = (bf16[4,128,256]{2,1,0:T(8,128)(2,1)S(1)}, bf16[4,128,256]{2,1,0:T(8,128)(2,1)S(1)}, u32[]{:S(2)}, u32[]{:S(2)}) collective-permute-start(bf16[4,128,256]{2,1,0:T(8,128)(2,1)S(1)} %collective-permute-done.1.refs_2_), channel_id=1, source_target_pairs={{0,56},{8,0},{16,8},{24,16},{32,24},{40,32},{48,40},{56,48},{1,57}... | collective-permute-start | bytes 786440 | tf_op jit(solution)/shard_map/ppermute | solution.py:25
  45.4 4.0 %collective-permute-done.5.refs_4_ = bf16[4,128,256]{2,1,0:T(8,128)(2,1)S(1)} collective-permute-done((bf16[4,128,256]{2,1,0:T(8,128)(2,1)S(1)}, bf16[4,128,256]{2,1,0:T(8,128)(2,1)S(1)}, u32[]{:S(2)}, u32[]{:S(2)}) %collective-permute-start.5) | collective-permute-done | bytes 262176 | tf_op jit(solution)/shard_map/ppermute | solution.py:25
  58.9 6.0 %views.1 = (bf16[4,512,256]{2,1,0:T(8,128)(2,1)}, bf16[4,512,256]{2,1,0:T(8,128)(2,1)}, f32[2,256,256]{2,1,0:T(8,128)}, bf16[272,256]{1,0:T(8,128)(2,1)}, bf16[272,256]{1,0:T(8,128)(2,1)}, /*index=5*/f32[8,256]{1,0:T(8,128)}) custom-call(s32[2]{0:T(128)} %pad_add_fusion.place_ref, bf16[4,4,2,64,512]{4,3,2,1,0:T(8,128)(2,1)} %bitcast.97, ...), custom_call_target="tpu_custom_call" | custom-call | tf_op jit(solution)/shard_map/views/pallas_call | solution.py:260
  100.4 3.9 %gram.1 = (bf16[2048,512]{1,0:T(8,128)(2,1)}, bf16[256,2176]{1,0:T(8,128)(2,1)}, f32[8,512]{1,0:T(8,128)}) custom-call(f32[1,1]{1,0:T(1,128)} %bitcast.11.diff_ref, bf16[144,512]{1,0:T(8,128)(2,1)} %copy-done.5, bf16[128,512]{1,0:T(8,128)(2,1)} %copy-done.8, bf16[144,512]{1,0:T(8,128)(2,1)} %copy-done.15, bf16[128,512]{1,0:T(8,128)(2,1)} %copy-done.21, ...), custom_call_target="tpu_custom_call" | custom-call | tf_op jit(solution)/shard_map/gram/pallas_call | solution.py:299
  104.3 6.7 %all-to-all-start.2 = ((bf16[16,16,2176]{2,1,0:T(8,128)(2,1)}), bf16[16,16,2176]{2,1,0:T(8,128)(2,1)S(1)}, u32[]{:S(2)}, u32[]{:S(2)}) async-start(bf16[16,16,2176]{2,1,0:T(8,128)(2,1)} %bitcast.105), calls=%async_computation.2 | async-start | bytes 2228224 | tf_op jit(solution)/shard_map/all_to_all | solution.py:29
  113.3 5.9 %turn.1 = (bf16[4,512,512]{2,1,0:T(8,128)(2,1)}, bf16[4,512,512]{2,1,0:T(8,128)(2,1)}, bf16[4,512,512]{2,1,0:T(8,128)(2,1)}) custom-call(bf16[4,4,2,64,512]{4,3,2,1,0:T(8,128)(2,1)} %bitcast.98, bf16[4,4,2,64,512]{4,3,2,1,0:T(8,128)(2,1)} %collective-permute-done.6.oth_ref, bf16[4,512,256]{2,1,0:T(8,128)(2,1)} %get-tuple-element.47.kept_ref, ...), custom_call_target="tpu_custom_call" | custom-call | tf_op jit(solution)/shard_map/turn/pallas_call | solution.py:322
  119.2 5.9 %all-to-all-done.2 = bf16[16,16,2176]{2,1,0:T(8,128)(2,1)S(1)} async-done(((bf16[16,16,2176]{2,1,0:T(8,128)(2,1)}), bf16[16,16,2176]{2,1,0:T(8,128)(2,1)S(1)}, u32[]{:S(2)}, u32[]{:S(2)}) %all-to-all-start.2) | async-done | bytes 1114144 | tf_op jit(solution)/shard_map/all_to_all | solution.py:29
  126.0 18.6 %all_to_all.30 = bf16[16,16,2048]{2,1,0:T(8,128)(2,1)S(1)} all-to-all(bf16[16,16,2048]{2,1,0:T(8,128)(2,1)S(1)} %broadcast_in_dim.5), channel_id=1, replica_groups=mesh['x'=4,'z'=8,'y'=4,'c'=2] {'x','y'}, dimensions={0} | all-to-all | bytes 2097152 | tf_op jit(solution)/shard_map/all_to_all | solution.py:29
  150.1 4.2 %far_terms.1 = (bf16[256,256]{1,0:T(8,128)(2,1)}, bf16[272,256]{1,0:T(8,128)(2,1)}) custom-call(s32[2]{0:T(128)} %pad_add_fusion.place_ref, bf16[4,512,512]{2,1,0:T(8,128)(2,1)} %get-tuple-element.52.own_ref, bf16[4,512,512]{2,1,0:T(8,128)(2,1)} %get-tuple-element.53.oth_ref, bf16[512,256]{1,0:T(8,128)(2,1)} %bitcast.101, f32[1,1]{1,0:T(1,128)} %bitcast.22.share_ref), custom_call_target="tpu_custom_call" | custom-call | tf_op jit(solution)/shard_map/far_terms/pallas_call | solution.py:364
  155.0 4.7 %input_terms.1 = bf16[4,512,512]{2,1,0:T(8,128)(2,1)} custom-call(bf16[512,256]{1,0:T(8,128)(2,1)} %bitcast.102, bf16[512,256]{1,0:T(8,128)(2,1)} %copy-done.13, bf16[4,512,512]{2,1,0:T(8,128)(2,1)} %get-tuple-element.61.w_ref), custom_call_target="tpu_custom_call" | custom-call | tf_op jit(solution)/shard_map/input_terms/pallas_call | solution.py:379
  159.7 5.1 %all-to-all-start.4 = ((bf16[16,2,64,512]{3,2,1,0:T(8,128)(2,1)}), bf16[16,2,64,512]{3,2,1,0:T(8,128)(2,1)S(1)}, u32[]{:S(2)}, u32[]{:S(2)}) async-start(bf16[16,2,64,512]{3,2,1,0:T(8,128)(2,1)} %bitcast.99), calls=%async_computation.4 | async-start | bytes 4194304 | tf_op jit(solution)/shard_map/all_to_all | solution.py:29
  166.9 4.7 %collective-permute-done.28 = bf16[256,256]{1,0:T(8,128)(2,1)S(1)} collective-permute-done((bf16[256,256]{1,0:T(8,128)(2,1)S(1)}, bf16[256,256]{1,0:T(8,128)(2,1)S(1)}, u32[]{:S(2)}, u32[]{:S(2)}) %collective-permute-start.28) | collective-permute-done | bytes 131104 | tf_op jit(solution)/shard_map/ppermute | solution.py:25
  171.6 5.4 %weight_terms.1 = bf16[8,528,256]{2,1,0:T(8,128)(2,1)} custom-call(s32[2]{0:T(128)} %pad_add_fusion.place_ref, bf16[4,512,512]{2,1,0:T(8,128)(2,1)} %get-tuple-element.52.own_ref, bf16[4,512,512]{2,1,0:T(8,128)(2,1)} %get-tuple-element.53.oth_ref, bf16[512,256]{1,0:T(8,128)(2,1)} %bitcast.103, f32[1,1]{1,0:T(1,128)} %bitcast.22.share_ref), custom_call_target="tpu_custom_call" | custom-call | tf_op jit(solution)/shard_map/weight_terms/pallas_call | solution.py:391
  181.4 5.6 %collective-permute-done.30 = bf16[528,256]{1,0:T(8,128)(2,1)S(1)} collective-permute-done((bf16[528,256]{1,0:T(8,128)(2,1)S(1)}, bf16[528,256]{1,0:T(8,128)(2,1)S(1)}, u32[]{:S(2)}, u32[]{:S(2)}) %collective-permute-start.30) | collective-permute-done | bytes 270368 | tf_op jit(solution)/shard_map/ppermute | solution.py:25
  191.5 4.7 %collective-permute-done.32 = bf16[528,256]{1,0:T(8,128)(2,1)S(1)} collective-permute-done((bf16[528,256]{1,0:T(8,128)(2,1)S(1)}, bf16[528,256]{1,0:T(8,128)(2,1)S(1)}, u32[]{:S(2)}, u32[]{:S(2)}) %collective-permute-start.32) | collective-permute-done | bytes 270368 | tf_op jit(solution)/shard_map/ppermute | solution.py:25
  200.7 4.4 %collective-permute-done.34 = bf16[528,256]{1,0:T(8,128)(2,1)S(1)} collective-permute-done((bf16[528,256]{1,0:T(8,128)(2,1)S(1)}, bf16[528,256]{1,0:T(8,128)(2,1)S(1)}, u32[]{:S(2)}, u32[]{:S(2)}) %collective-permute-start.34) | collective-permute-done | bytes 270368 | tf_op jit(solution)/shard_map/ppermute | solution.py:25
  207.0 4.3 %all-to-all-start.5 = ((bf16[4,128,256]{2,1,0:T(8,128)(2,1)}), bf16[4,128,256]{2,1,0:T(8,128)(2,1)S(1)}, u32[]{:S(2)}, u32[]{:S(2)}) async-start(bf16[4,128,256]{2,1,0:T(8,128)(2,1)} %bitcast.30), calls=%async_computation.5 | async-start | bytes 524288 | tf_op jit(solution)/shard_map/all_to_all | solution.py:29
  (170 shorter events, 83.6 us)
Async XLA Ops:
  2.3 11.0 %all-to-all-start = ((bf16[4,128,256]{2,1,0:T(8,128)(2,1)}), bf16[4,128,256]{2,1,0:T(8,128)(2,1)S(1)}, u32[]{:S(2)}, u32[]{:S(2)}) async-start(bf16[4,128,256]{2,1,0:T(8,128)(2,1)} %pad_maximum_fusion), calls=%async_computation | async-start | bytes 524288 | tf_op jit(solution)/shard_map/all_to_all | solution.py:29
  14.9 34.5 %all-to-all-start.1 = ((bf16[16,2,64,512]{3,2,1,0:T(8,128)(2,1)}), bf16[16,2,64,512]{3,2,1,0:T(8,128)(2,1)S(1)}, u32[]{:S(2)}, u32[]{:S(2)}) async-start(bf16[16,2,64,512]{3,2,1,0:T(8,128)(2,1)} %broadcast_in_dim.4), calls=%async_computation.1 | async-start | bytes 4194304 | tf_op jit(solution)/shard_map/all_to_all | solution.py:29
  20.4 9.7 %collective-permute-start = (bf16[4,128,256]{2,1,0:T(8,128)(2,1)S(1)}, bf16[4,128,256]{2,1,0:T(8,128)(2,1)S(1)}, u32[]{:S(2)}, u32[]{:S(2)}) collective-permute-start(bf16[4,128,256]{2,1,0:T(8,128)(2,1)S(1)} %all-to-all-done.refs_0_), channel_id=1, source_target_pairs={{0,56},{8,0},{16,8},{24,16},{32,24},{40,32},{48,40},{56,48},{1,57}... | collective-permute-start | bytes 786440 | tf_op jit(solution)/shard_map/ppermute | solution.py:25
  33.8 7.9 %collective-permute-start.4 = (bf16[4,128,256]{2,1,0:T(8,128)(2,1)S(1)}, bf16[4,128,256]{2,1,0:T(8,128)(2,1)S(1)}, u32[]{:S(2)}, u32[]{:S(2)}) collective-permute-start(bf16[4,128,256]{2,1,0:T(8,128)(2,1)S(1)} %collective-permute-done.3.refs_6_), channel_id=1, source_target_pairs={{0,8},{8,16},{16,24},{24,32},{32,40},{40,48},{48,56},{56,0},{1,9},... | collective-permute-start | bytes 786440 | tf_op jit(solution)/shard_map/ppermute | solution.py:25
  49.3 8.9 %collective-permute-start.6 = (bf16[4,4,2,64,512]{4,3,2,1,0:T(8,128)(2,1)S(1)}, bf16[4,4,2,64,512]{4,3,2,1,0:T(8,128)(2,1)}, u32[]{:S(2)}, u32[]{:S(2)}) collective-permute-start(bf16[4,4,2,64,512]{4,3,2,1,0:T(8,128)(2,1)S(1)} %bitcast.96), channel_id=1, source_target_pairs={{0,1},{1,0},{2,3},{3,2},{4,5},{5,4},{6,7},{7,6},{8,9},{9,8},{10,11... | collective-permute-start | bytes 6291464 | tf_op jit(solution)/shard_map/ppermute | solution.py:21
  50.3 8.0 %collective-permute-start.7 = (bf16[2,128,256]{2,1,0:T(8,128)(2,1)}, bf16[2,128,256]{2,1,0:T(8,128)(2,1)S(1)}, u32[]{:S(2)}, u32[]{:S(2)}) collective-permute-start(bf16[2,128,256]{2,1,0:T(8,128)(2,1)} %slice.141), channel_id=1, source_target_pairs={{0,8},{8,16},{16,24},{24,32},{32,40},{40,48},{48,56},{56,0},{1,9},... | collective-permute-start | bytes 393224 | tf_op jit(solution)/shard_map/ppermute | solution.py:25
  66.7 9.3 %collective-permute-start.11 = (bf16[128,512]{1,0:T(8,128)(2,1)S(1)}, bf16[128,512]{1,0:T(8,128)(2,1)S(1)}, u32[]{:S(2)}, u32[]{:S(2)}) collective-permute-start(bf16[128,512]{1,0:T(8,128)(2,1)S(1)} %slice.144.refs_1_), channel_id=1, source_target_pairs={{0,56},{8,0},{16,8},{24,16},{32,24},{40,32},{48,40},{56,48},{1,57}... | collective-permute-start | bytes 393224 | tf_op jit(solution)/shard_map/ppermute | solution.py:25
  74.0 7.8 %collective-permute-start.17 = (bf16[144,512]{1,0:T(8,128)(2,1)S(1)}, bf16[144,512]{1,0:T(8,128)(2,1)S(1)}, u32[]{:S(2)}, u32[]{:S(2)}) collective-permute-start(bf16[144,512]{1,0:T(8,128)(2,1)S(1)} %collective-permute-done.16.refs_14_), channel_id=1, source_target_pairs={{0,8},{8,16},{16,24},{24,32},{32,40},{40,48},{48,56},{56,0},{1,9},... | collective-permute-start | bytes 442376 | tf_op jit(solution)/shard_map/ppermute | solution.py:25
  74.0 9.6 %collective-permute-start.21 = (bf16[128,512]{1,0:T(8,128)(2,1)S(1)}, bf16[128,512]{1,0:T(8,128)(2,1)S(1)}, u32[]{:S(2)}, u32[]{:S(2)}) collective-permute-start(bf16[128,512]{1,0:T(8,128)(2,1)S(1)} %slice.144.refs_1_), channel_id=1, source_target_pairs={{0,8},{8,16},{16,24},{24,32},{32,40},{40,48},{48,56},{56,0},{1,9},... | collective-permute-start | bytes 393224 | tf_op jit(solution)/shard_map/ppermute | solution.py:25
  77.6 12.4 %collective-permute-start.12 = (bf16[144,512]{1,0:T(8,128)(2,1)S(1)}, bf16[144,512]{1,0:T(8,128)(2,1)S(1)}, u32[]{:S(2)}, u32[]{:S(2)}) collective-permute-start(bf16[144,512]{1,0:T(8,128)(2,1)S(1)} %collective-permute-done.10.refs_2_), channel_id=1, source_target_pairs={{0,56},{8,0},{16,8},{24,16},{32,24},{40,32},{48,40},{56,48},{1,57}... | collective-permute-start | bytes 442376 | tf_op jit(solution)/shard_map/ppermute | solution.py:25
  81.8 11.6 %collective-permute-start.18 = (bf16[144,512]{1,0:T(8,128)(2,1)S(1)}, bf16[144,512]{1,0:T(8,128)(2,1)S(1)}, u32[]{:S(2)}, u32[]{:S(2)}) collective-permute-start(bf16[144,512]{1,0:T(8,128)(2,1)S(1)} %collective-permute-done.17.refs_12_), channel_id=1, source_target_pairs={{0,8},{8,16},{16,24},{24,32},{32,40},{40,48},{48,56},{56,0},{1,9},... | collective-permute-start | bytes 442376 | tf_op jit(solution)/shard_map/ppermute | solution.py:25
  83.6 9.7 %collective-permute-start.15 = (bf16[128,512]{1,0:T(8,128)(2,1)S(1)}, bf16[128,512]{1,0:T(8,128)(2,1)S(1)}, u32[]{:S(2)}, u32[]{:S(2)}) collective-permute-start(bf16[128,512]{1,0:T(8,128)(2,1)S(1)} %collective-permute-done.13.refs_5_), channel_id=1, source_target_pairs={{0,56},{8,0},{16,8},{24,16},{32,24},{40,32},{48,40},{56,48},{1,57}... | collective-permute-start | bytes 393224 | tf_op jit(solution)/shard_map/ppermute | solution.py:25
  86.9 25.4 %collective-permute-start.25 = (bf16[4,512,256]{2,1,0:T(8,128)(2,1)}, bf16[4,512,256]{2,1,0:T(8,128)(2,1)S(1)}, u32[]{:S(2)}, u32[]{:S(2)}) collective-permute-start(bf16[4,512,256]{2,1,0:T(8,128)(2,1)} %get-tuple-element.48), channel_id=1, source_target_pairs={{0,1},{1,0},{2,3},{3,2},{4,5},{5,4},{6,7},{7,6},{8,9},{9,8},{10,11... | collective-permute-start | bytes 3145736 | tf_op jit(solution)/shard_map/ppermute | solution.py:21
  90.1 8.4 %collective-permute-start.23 = (bf16[128,512]{1,0:T(8,128)(2,1)S(1)}, bf16[128,512]{1,0:T(8,128)(2,1)S(1)}, u32[]{:S(2)}, u32[]{:S(2)}) collective-permute-start(bf16[128,512]{1,0:T(8,128)(2,1)S(1)} %collective-permute-done.22.refs_13_), channel_id=1, source_target_pairs={{0,8},{8,16},{16,24},{24,32},{32,40},{40,48},{48,56},{56,0},{1,9},... | collective-permute-start | bytes 393224 | tf_op jit(solution)/shard_map/ppermute | solution.py:25
  90.1 8.4 %collective-permute-start.14 = (bf16[144,512]{1,0:T(8,128)(2,1)S(1)}, bf16[144,512]{1,0:T(8,128)(2,1)S(1)}, u32[]{:S(2)}, u32[]{:S(2)}) collective-permute-start(bf16[144,512]{1,0:T(8,128)(2,1)S(1)} %collective-permute-done.12.refs_4_), channel_id=1, source_target_pairs={{0,56},{8,0},{16,8},{24,16},{32,24},{40,32},{48,40},{56,48},{1,57}... | collective-permute-start | bytes 442376 | tf_op jit(solution)/shard_map/ppermute | solution.py:25
  104.3 20.8 %all-to-all-start.2 = ((bf16[16,16,2176]{2,1,0:T(8,128)(2,1)}), bf16[16,16,2176]{2,1,0:T(8,128)(2,1)S(1)}, u32[]{:S(2)}, u32[]{:S(2)}) async-start(bf16[16,16,2176]{2,1,0:T(8,128)(2,1)} %bitcast.105), calls=%async_computation.2 | async-start | bytes 2228224 | tf_op jit(solution)/shard_map/all_to_all | solution.py:29
  154.2 17.4 %collective-permute-start.29 = (bf16[272,256]{1,0:T(8,128)(2,1)}, bf16[272,256]{1,0:T(8,128)(2,1)S(1)}, u32[]{:S(2)}, u32[]{:S(2)}) collective-permute-start(bf16[272,256]{1,0:T(8,128)(2,1)} %get-tuple-element.59), channel_id=1, source_target_pairs={{0,56},{8,0},{16,8},{24,16},{32,24},{40,32},{48,40},{56,48},{1,57}... | collective-permute-start | bytes 417800 | tf_op jit(solution)/shard_map/ppermute | solution.py:25
  159.7 47.2 %all-to-all-start.4 = ((bf16[16,2,64,512]{3,2,1,0:T(8,128)(2,1)}), bf16[16,2,64,512]{3,2,1,0:T(8,128)(2,1)S(1)}, u32[]{:S(2)}, u32[]{:S(2)}) async-start(bf16[16,2,64,512]{3,2,1,0:T(8,128)(2,1)} %bitcast.99), calls=%async_computation.4 | async-start | bytes 4194304 | tf_op jit(solution)/shard_map/all_to_all | solution.py:29
  178.1 8.9 %collective-permute-start.30 = (bf16[528,256]{1,0:T(8,128)(2,1)S(1)}, bf16[528,256]{1,0:T(8,128)(2,1)S(1)}, u32[]{:S(2)}, u32[]{:S(2)}) collective-permute-start(bf16[528,256]{1,0:T(8,128)(2,1)S(1)} %get-tuple-element.81), channel_id=1, source_target_pairs={{0,8},{8,16},{16,24},{24,32},{32,40},{40,48},{48,56},{56,0},{1,9},... | collective-permute-start | bytes 811016 | tf_op jit(solution)/shard_map/ppermute | solution.py:25
  178.7 8.3 %collective-permute-start.31 = (bf16[528,256]{1,0:T(8,128)(2,1)S(1)}, bf16[528,256]{1,0:T(8,128)(2,1)S(1)}, u32[]{:S(2)}, u32[]{:S(2)}) collective-permute-start(bf16[528,256]{1,0:T(8,128)(2,1)S(1)} %get-tuple-element.80), channel_id=1, source_target_pairs={{0,56},{8,0},{16,8},{24,16},{32,24},{40,32},{48,40},{56,48},{1,57}... | collective-permute-start | bytes 811016 | tf_op jit(solution)/shard_map/ppermute | solution.py:25
  188.2 8.0 %collective-permute-start.32 = (bf16[528,256]{1,0:T(8,128)(2,1)S(1)}, bf16[528,256]{1,0:T(8,128)(2,1)S(1)}, u32[]{:S(2)}, u32[]{:S(2)}) collective-permute-start(bf16[528,256]{1,0:T(8,128)(2,1)S(1)} %get-tuple-element.79), channel_id=1, source_target_pairs={{0,8},{8,16},{16,24},{24,32},{32,40},{40,48},{48,56},{56,0},{1,9},... | collective-permute-start | bytes 811016 | tf_op jit(solution)/shard_map/ppermute | solution.py:25
  188.3 8.0 %collective-permute-start.33 = (bf16[528,256]{1,0:T(8,128)(2,1)S(1)}, bf16[528,256]{1,0:T(8,128)(2,1)S(1)}, u32[]{:S(2)}, u32[]{:S(2)}) collective-permute-start(bf16[528,256]{1,0:T(8,128)(2,1)S(1)} %get-tuple-element.78), channel_id=1, source_target_pairs={{0,56},{8,0},{16,8},{24,16},{32,24},{40,32},{48,40},{56,48},{1,57}... | collective-permute-start | bytes 811016 | tf_op jit(solution)/shard_map/ppermute | solution.py:25
  197.4 7.7 %collective-permute-start.34 = (bf16[528,256]{1,0:T(8,128)(2,1)S(1)}, bf16[528,256]{1,0:T(8,128)(2,1)S(1)}, u32[]{:S(2)}, u32[]{:S(2)}) collective-permute-start(bf16[528,256]{1,0:T(8,128)(2,1)S(1)} %get-tuple-element.76), channel_id=1, source_target_pairs={{0,8},{8,16},{16,24},{24,32},{32,40},{40,48},{48,56},{56,0},{1,9},... | collective-permute-start | bytes 811016 | tf_op jit(solution)/shard_map/ppermute | solution.py:25
  207.0 10.9 %all-to-all-start.5 = ((bf16[4,128,256]{2,1,0:T(8,128)(2,1)}), bf16[4,128,256]{2,1,0:T(8,128)(2,1)S(1)}, u32[]{:S(2)}, u32[]{:S(2)}) async-start(bf16[4,128,256]{2,1,0:T(8,128)(2,1)} %bitcast.30), calls=%async_computation.5 | async-start | bytes 524288 | tf_op jit(solution)/shard_map/all_to_all | solution.py:29
  (50 other events, 488.4 us)

commit v2 on v1

--- a/solution.py
+++ b/solution.py
@@ -86,9 +86,9 @@
     return pl.BlockSpec(shape, lambda j: tuple(j if d == dim else 0 for d in range(len(shape))))
 
 
-def flat_rows(ref):
+def flat_rows(ref, y=0):
     nx, _, nv, rows, width = ref.shape
-    return ref[:, 0].reshape(nx * nv * rows, width)
+    return ref[:, y].reshape(nx * nv * rows, width)
 
 
 def views_kernel(place_ref, own_ref, oth_ref, *refs):
@@ -188,9 +188,9 @@
     rows = NY * kz
     for ref, lead in ((own_ref, core), (oth_ref, 1 - core)):
         term = dot(ref[0], g_ref[...], 1, 0).astype(BF)
+        place = pl.ds(pl.multiple_of(step * kz, kz), kz)
         for q in range(HALF):
-            k = lax.rem(lead * HALF + q - zi + NZ, NZ)
-            out_ref[k, pl.ds(pl.multiple_of(step * kz, kz), kz)] = term[q * kz : (q + 1) * kz]
+            out_ref[lax.rem(lead * HALF + q - zi + NZ, NZ), place] = term[q * kz : (q + 1) * kz]
 
     @pl.when(step == 0)
     def _():
@@ -202,28 +202,17 @@
 
 
 def far_kernel(place_ref, own_ref, oth_ref, g_ref, share_ref, a_ref, b_ref):
-    step = pl.program_id(0)
     core = place_ref[0]
     zi = place_ref[1]
     kz = own_ref.shape[1]
     mine = 1 - zi // HALF == core
-    block = jnp.where(mine, own_ref[0].astype(F32), oth_ref[0].astype(F32)).astype(BF)
-    term = dot(block, g_ref[...], 1, 0).astype(BF)
-    place = pl.ds(pl.multiple_of(lax.rem(step, NY // 2) * kz, kz), kz)
-
-    @pl.when(step < NY // 2)
-    def _():
-        a_ref[place] = term
-
-    @pl.when(step >= NY // 2)
-    def _():
-        b_ref[place] = term
-
-    @pl.when(step == 0)
-    def _():
-        row = lax.broadcasted_iota(jnp.int32, (STAT, b_ref.shape[1]), 0)
-        lane = lax.broadcasted_iota(jnp.int32, (STAT, b_ref.shape[1]), 1)
-        b_ref[NY // 2 * kz :] = in_lanes(share_ref[...], lane, 3 * zi, row == 0).astype(BF)
+    block = jnp.where(mine, own_ref[...].astype(F32), oth_ref[...].astype(F32)).astype(BF)
+    term = dot(block.reshape(NY * kz, own_ref.shape[2]), g_ref[...], 1, 0).astype(BF)
+    a_ref[...] = term[: NY // 2 * kz]
+    b_ref[: NY // 2 * kz] = term[NY // 2 * kz :]
+    row = lax.broadcasted_iota(jnp.int32, (STAT, b_ref.shape[1]), 0)
+    lane = lax.broadcasted_iota(jnp.int32, (STAT, b_ref.shape[1]), 1)
+    b_ref[NY // 2 * kz :] = in_lanes(share_ref[...], lane, 3 * zi, row == 0).astype(BF)
 
 
 def input_kernel(own_ref, oth_ref, w_ref, out_ref):
@@ -358,14 +347,14 @@
     grad_views = (inv_grad + hinge_grad + cov_grad).astype(BF)
     grads = grad_views.reshape(2, NX, rows, sub).transpose(1, 0, 2, 3).reshape(flat, sub)
 
-    far_block = pl.BlockSpec((1, kz, flat), lambda j, place: (j, lax.rem(place[1], HALF), 0))
+    far_block = pl.BlockSpec((NY, kz, flat), lambda j, place: (0, lax.rem(place[1], HALF), 0))
     held = lambda s: pl.BlockSpec(s, lambda j, place: (0,) * len(s))
     half = NX // 2 * kz
     far_right, far_left = pl.pallas_call(
         far_kernel,
         grid_spec=pltpu.PrefetchScalarGridSpec(
             num_scalar_prefetch=1,
-            grid=(NY,),
+            grid=(1,),
             in_specs=[far_block, far_block, held((flat, sub)), held((1, 1))],
             out_specs=[held((half, sub)), held((half + STAT, sub))],
         ),

time: 221 us -> 220 us (level)
  transfers between devices with their start and end apart: 42 -> 42, of which waited for: 22 -> 22; matrix products, arithmetic and copies ran while one was open for 7% -> 7% of each run, Pallas kernels for 11% -> 10%
where the time goes in v2:
time: 220 us; the launch traced here: 219 us
  starting transfers between devices  75.4 us (34%)
  waiting for transfers between devices  66.8 us (30%)
  Pallas kernels  28.8 us (13%)
  blocking collectives  18.6 us (8%)
  other arithmetic  13.1 us (6%)
  local copies, waits for them, and re-layouts  9.62 us (4%)
  between operations  5.55 us (3%)
    ppermute x30, starting transfers between devices, hop(): return lax.ppermute(v, 'z', [(i, (i + k) % NZ) for i in range(NZ)])  48.7 us
    ppermute x30, waiting for transfers between devices, hop(): return lax.ppermute(v, 'z', [(i, (i + k) % NZ) for i in range(NZ)])  48.3 us
    all_to_all x5, starting transfers between devices, exchange(): return lax.all_to_all(v, axes, split_axis=0, concat_axis=0, tiled=True)  25.9 us
    all_to_all x1, blocking collectives, exchange(): return lax.all_to_all(v, axes, split_axis=0, concat_axis=0, tiled=True)  18.6 us
    all_to_all x5, waiting for transfers between devices, exchange(): return lax.all_to_all(v, axes, split_axis=0, concat_axis=0, tiled=True)  15.1 us
    pallas_call x1, Pallas kernels, on_device(): pl.pallas_call(views_kernel, grid=(NY,), in_specs=[smem, at_dim(hblock, 1...  5.98 us
    pallas_call x1, Pallas kernels, on_device(): pl.pallas_call(turn_kernel, grid=(NY,), in_specs=[at_dim(hblock, 1), at_d...  5.87 us
    pallas_call x1, Pallas kernels, on_device(): pl.pallas_call(weight_kernel, grid=(NY,), in_specs=[smem] + [at_dim((1, k...  5.39 us
  transfers between devices with their start and end apart: 42, of which 22 were waited for; matrix products, arithmetic and copies ran while one was open for 7% of the time, Pallas kernels for 10%

profile of v2, /device:TPU:8, one launch (start us, length us, event | category | flops | bytes accessed | tf_op | source)
XLA Modules:
  0.0 218.5 jit_solution(7680379449718993465)
XLA Ops:
  2.3 4.3 %all-to-all-start = ((bf16[4,128,256]{2,1,0:T(8,128)(2,1)}), bf16[4,128,256]{2,1,0:T(8,128)(2,1)S(1)}, u32[]{:S(2)}, u32[]{:S(2)}) async-start(bf16[4,128,256]{2,1,0:T(8,128)(2,1)} %pad_maximum_fusion), calls=%async_computation | async-start | bytes 524288 | tf_op jit(solution)/shard_map/all_to_all | solution.py:29
  7.5 5.8 %all-to-all-done.refs_0_ = bf16[4,128,256]{2,1,0:T(8,128)(2,1)S(1)} async-done(((bf16[4,128,256]{2,1,0:T(8,128)(2,1)}), bf16[4,128,256]{2,1,0:T(8,128)(2,1)S(1)}, u32[]{:S(2)}, u32[]{:S(2)}) %all-to-all-start) | async-done | bytes 262176 | tf_op jit(solution)/shard_map/all_to_all | solution.py:29
  14.9 5.5 %all-to-all-start.1 = ((bf16[16,2,64,512]{3,2,1,0:T(8,128)(2,1)}), bf16[16,2,64,512]{3,2,1,0:T(8,128)(2,1)S(1)}, u32[]{:S(2)}, u32[]{:S(2)}) async-start(bf16[16,2,64,512]{3,2,1,0:T(8,128)(2,1)} %broadcast_in_dim.4), calls=%async_computation.1 | async-start | bytes 4194304 | tf_op jit(solution)/shard_map/all_to_all | solution.py:29
  20.4 5.9 %collective-permute-start = (bf16[4,128,256]{2,1,0:T(8,128)(2,1)S(1)}, bf16[4,128,256]{2,1,0:T(8,128)(2,1)S(1)}, u32[]{:S(2)}, u32[]{:S(2)}) collective-permute-start(bf16[4,128,256]{2,1,0:T(8,128)(2,1)S(1)} %all-to-all-done.refs_0_), channel_id=1, source_target_pairs={{0,56},{8,0},{16,8},{24,16},{32,24},{40,32},{48,40},{56,48},{1,57}... | collective-permute-start | bytes 786440 | tf_op jit(solution)/shard_map/ppermute | solution.py:25
  26.3 3.9 %collective-permute-done.refs_1_ = bf16[4,128,256]{2,1,0:T(8,128)(2,1)S(1)} collective-permute-done((bf16[4,128,256]{2,1,0:T(8,128)(2,1)S(1)}, bf16[4,128,256]{2,1,0:T(8,128)(2,1)S(1)}, u32[]{:S(2)}, u32[]{:S(2)}) %collective-permute-start) | collective-permute-done | bytes 262176 | tf_op jit(solution)/shard_map/ppermute | solution.py:25
  30.1 3.7 %collective-permute-start.1 = (bf16[4,128,256]{2,1,0:T(8,128)(2,1)S(1)}, bf16[4,128,256]{2,1,0:T(8,128)(2,1)S(1)}, u32[]{:S(2)}, u32[]{:S(2)}) collective-permute-start(bf16[4,128,256]{2,1,0:T(8,128)(2,1)S(1)} %collective-permute-done.refs_1_), channel_id=1, source_target_pairs={{0,56},{8,0},{16,8},{24,16},{32,24},{40,32},{48,40},{56,48},{1,57}... | collective-permute-start | bytes 786440 | tf_op jit(solution)/shard_map/ppermute | solution.py:25
  33.8 3.9 %collective-permute-done.1.refs_2_ = bf16[4,128,256]{2,1,0:T(8,128)(2,1)S(1)} collective-permute-done((bf16[4,128,256]{2,1,0:T(8,128)(2,1)S(1)}, bf16[4,128,256]{2,1,0:T(8,128)(2,1)S(1)}, u32[]{:S(2)}, u32[]{:S(2)}) %collective-permute-start.1) | collective-permute-done | bytes 262176 | tf_op jit(solution)/shard_map/ppermute | solution.py:25
  37.7 3.7 %collective-permute-start.2 = (bf16[4,128,256]{2,1,0:T(8,128)(2,1)S(1)}, bf16[4,128,256]{2,1,0:T(8,128)(2,1)S(1)}, u32[]{:S(2)}, u32[]{:S(2)}) collective-permute-start(bf16[4,128,256]{2,1,0:T(8,128)(2,1)S(1)} %collective-permute-done.1.refs_2_), channel_id=1, source_target_pairs={{0,56},{8,0},{16,8},{24,16},{32,24},{40,32},{48,40},{56,48},{1,57}... | collective-permute-start | bytes 786440 | tf_op jit(solution)/shard_map/ppermute | solution.py:25
  45.4 4.0 %collective-permute-done.5.refs_4_ = bf16[4,128,256]{2,1,0:T(8,128)(2,1)S(1)} collective-permute-done((bf16[4,128,256]{2,1,0:T(8,128)(2,1)S(1)}, bf16[4,128,256]{2,1,0:T(8,128)(2,1)S(1)}, u32[]{:S(2)}, u32[]{:S(2)}) %collective-permute-start.5) | collective-permute-done | bytes 262176 | tf_op jit(solution)/shard_map/ppermute | solution.py:25
  50.9 3.7 %collective-permute-start.8 = (bf16[2,128,256]{2,1,0:T(8,128)(2,1)}, bf16[2,128,256]{2,1,0:T(8,128)(2,1)}, u32[]{:S(2)}, u32[]{:S(2)}) collective-permute-start(bf16[2,128,256]{2,1,0:T(8,128)(2,1)} %slice.142), channel_id=1, source_target_pairs={{0,56},{8,0},{16,8},{24,16},{32,24},{40,32},{48,40},{56,48},{1,57}... | collective-permute-start | bytes 393224 | tf_op jit(solution)/shard_map/ppermute | solution.py:25
  58.9 6.0 %views.1 = (bf16[4,512,256]{2,1,0:T(8,128)(2,1)}, bf16[4,512,256]{2,1,0:T(8,128)(2,1)}, f32[2,256,256]{2,1,0:T(8,128)}, bf16[272,256]{1,0:T(8,128)(2,1)}, bf16[272,256]{1,0:T(8,128)(2,1)}, /*index=5*/f32[8,256]{1,0:T(8,128)}) custom-call(s32[2]{0:T(128)} %pad_add_fusion.place_ref, bf16[4,4,2,64,512]{4,3,2,1,0:T(8,128)(2,1)} %bitcast.97, ...), custom_call_target="tpu_custom_call" | custom-call | tf_op jit(solution)/shard_map/views/pallas_call | solution.py:249
  100.4 3.9 %gram.1 = (bf16[2048,512]{1,0:T(8,128)(2,1)}, bf16[256,2176]{1,0:T(8,128)(2,1)}, f32[8,512]{1,0:T(8,128)}) custom-call(f32[1,1]{1,0:T(1,128)} %bitcast.11.diff_ref, bf16[144,512]{1,0:T(8,128)(2,1)} %copy-done.5, bf16[128,512]{1,0:T(8,128)(2,1)} %copy-done.8, bf16[144,512]{1,0:T(8,128)(2,1)} %copy-done.15, bf16[128,512]{1,0:T(8,128)(2,1)} %copy-done.21, ...), custom_call_target="tpu_custom_call" | custom-call | tf_op jit(solution)/shard_map/gram/pallas_call | solution.py:288
  104.3 6.7 %all-to-all-start.2 = ((bf16[16,16,2176]{2,1,0:T(8,128)(2,1)}), bf16[16,16,2176]{2,1,0:T(8,128)(2,1)S(1)}, u32[]{:S(2)}, u32[]{:S(2)}) async-start(bf16[16,16,2176]{2,1,0:T(8,128)(2,1)} %bitcast.105), calls=%async_computation.2 | async-start | bytes 2228224 | tf_op jit(solution)/shard_map/all_to_all | solution.py:29
  113.3 5.9 %turn.1 = (bf16[4,512,512]{2,1,0:T(8,128)(2,1)}, bf16[4,512,512]{2,1,0:T(8,128)(2,1)}, bf16[4,512,512]{2,1,0:T(8,128)(2,1)}) custom-call(bf16[4,4,2,64,512]{4,3,2,1,0:T(8,128)(2,1)} %bitcast.98, bf16[4,4,2,64,512]{4,3,2,1,0:T(8,128)(2,1)} %collective-permute-done.6.oth_ref, bf16[4,512,256]{2,1,0:T(8,128)(2,1)} %get-tuple-element.47.kept_ref, ...), custom_call_target="tpu_custom_call" | custom-call | tf_op jit(solution)/shard_map/turn/pallas_call | solution.py:311
  119.2 5.9 %all-to-all-done.2 = bf16[16,16,2176]{2,1,0:T(8,128)(2,1)S(1)} async-done(((bf16[16,16,2176]{2,1,0:T(8,128)(2,1)}), bf16[16,16,2176]{2,1,0:T(8,128)(2,1)S(1)}, u32[]{:S(2)}, u32[]{:S(2)}) %all-to-all-start.2) | async-done | bytes 1114144 | tf_op jit(solution)/shard_map/all_to_all | solution.py:29
  126.0 18.6 %all_to_all.30 = bf16[16,16,2048]{2,1,0:T(8,128)(2,1)S(1)} all-to-all(bf16[16,16,2048]{2,1,0:T(8,128)(2,1)S(1)} %broadcast_in_dim.5), channel_id=1, replica_groups=mesh['x'=4,'z'=8,'y'=4,'c'=2] {'x','y'}, dimensions={0} | all-to-all | bytes 2097152 | tf_op jit(solution)/shard_map/all_to_all | solution.py:29
  153.7 4.7 %input_terms.1 = bf16[4,512,512]{2,1,0:T(8,128)(2,1)} custom-call(bf16[512,256]{1,0:T(8,128)(2,1)} %bitcast.102, bf16[512,256]{1,0:T(8,128)(2,1)} %copy-done.13, bf16[4,512,512]{2,1,0:T(8,128)(2,1)} %get-tuple-element.61.w_ref), custom_call_target="tpu_custom_call" | custom-call | tf_op jit(solution)/shard_map/input_terms/pallas_call | solution.py:368
  158.5 5.1 %all-to-all-start.4 = ((bf16[16,2,64,512]{3,2,1,0:T(8,128)(2,1)}), bf16[16,2,64,512]{3,2,1,0:T(8,128)(2,1)S(1)}, u32[]{:S(2)}, u32[]{:S(2)}) async-start(bf16[16,2,64,512]{3,2,1,0:T(8,128)(2,1)} %bitcast.99), calls=%async_computation.4 | async-start | bytes 4194304 | tf_op jit(solution)/shard_map/all_to_all | solution.py:29
  165.7 4.7 %collective-permute-done.28 = bf16[256,256]{1,0:T(8,128)(2,1)S(1)} collective-permute-done((bf16[256,256]{1,0:T(8,128)(2,1)S(1)}, bf16[256,256]{1,0:T(8,128)(2,1)S(1)}, u32[]{:S(2)}, u32[]{:S(2)}) %collective-permute-start.28) | collective-permute-done | bytes 131104 | tf_op jit(solution)/shard_map/ppermute | solution.py:25
  170.4 5.4 %weight_terms.1 = bf16[8,528,256]{2,1,0:T(8,128)(2,1)} custom-call(s32[2]{0:T(128)} %pad_add_fusion.place_ref, bf16[4,512,512]{2,1,0:T(8,128)(2,1)} %get-tuple-element.52.own_ref, bf16[4,512,512]{2,1,0:T(8,128)(2,1)} %get-tuple-element.53.oth_ref, bf16[512,256]{1,0:T(8,128)(2,1)} %bitcast.103, f32[1,1]{1,0:T(1,128)} %bitcast.22.share_ref), custom_call_target="tpu_custom_call" | custom-call | tf_op jit(solution)/shard_map/weight_terms/pallas_call | solution.py:380
  180.2 5.6 %collective-permute-done.30 = bf16[528,256]{1,0:T(8,128)(2,1)S(1)} collective-permute-done((bf16[528,256]{1,0:T(8,128)(2,1)S(1)}, bf16[528,256]{1,0:T(8,128)(2,1)S(1)}, u32[]{:S(2)}, u32[]{:S(2)}) %collective-permute-start.30) | collective-permute-done | bytes 270368 | tf_op jit(solution)/shard_map/ppermute | solution.py:25
  190.2 4.7 %collective-permute-done.32 = bf16[528,256]{1,0:T(8,128)(2,1)S(1)} collective-permute-done((bf16[528,256]{1,0:T(8,128)(2,1)S(1)}, bf16[528,256]{1,0:T(8,128)(2,1)S(1)}, u32[]{:S(2)}, u32[]{:S(2)}) %collective-permute-start.32) | collective-permute-done | bytes 270368 | tf_op jit(solution)/shard_map/ppermute | solution.py:25
  199.5 4.4 %collective-permute-done.34 = bf16[528,256]{1,0:T(8,128)(2,1)S(1)} collective-permute-done((bf16[528,256]{1,0:T(8,128)(2,1)S(1)}, bf16[528,256]{1,0:T(8,128)(2,1)S(1)}, u32[]{:S(2)}, u32[]{:S(2)}) %collective-permute-start.34) | collective-permute-done | bytes 270368 | tf_op jit(solution)/shard_map/ppermute | solution.py:25
  205.7 4.3 %all-to-all-start.5 = ((bf16[4,128,256]{2,1,0:T(8,128)(2,1)}), bf16[4,128,256]{2,1,0:T(8,128)(2,1)S(1)}, u32[]{:S(2)}, u32[]{:S(2)}) async-start(bf16[4,128,256]{2,1,0:T(8,128)(2,1)} %bitcast.30), calls=%async_computation.5 | async-start | bytes 524288 | tf_op jit(solution)/shard_map/all_to_all | solution.py:29
  (170 shorter events, 82.8 us)
Async XLA Ops:
  2.3 11.0 %all-to-all-start = ((bf16[4,128,256]{2,1,0:T(8,128)(2,1)}), bf16[4,128,256]{2,1,0:T(8,128)(2,1)S(1)}, u32[]{:S(2)}, u32[]{:S(2)}) async-start(bf16[4,128,256]{2,1,0:T(8,128)(2,1)} %pad_maximum_fusion), calls=%async_computation | async-start | bytes 524288 | tf_op jit(solution)/shard_map/all_to_all | solution.py:29
  14.9 34.5 %all-to-all-start.1 = ((bf16[16,2,64,512]{3,2,1,0:T(8,128)(2,1)}), bf16[16,2,64,512]{3,2,1,0:T(8,128)(2,1)S(1)}, u32[]{:S(2)}, u32[]{:S(2)}) async-start(bf16[16,2,64,512]{3,2,1,0:T(8,128)(2,1)} %broadcast_in_dim.4), calls=%async_computation.1 | async-start | bytes 4194304 | tf_op jit(solution)/shard_map/all_to_all | solution.py:29
  20.4 9.7 %collective-permute-start = (bf16[4,128,256]{2,1,0:T(8,128)(2,1)S(1)}, bf16[4,128,256]{2,1,0:T(8,128)(2,1)S(1)}, u32[]{:S(2)}, u32[]{:S(2)}) collective-permute-start(bf16[4,128,256]{2,1,0:T(8,128)(2,1)S(1)} %all-to-all-done.refs_0_), channel_id=1, source_target_pairs={{0,56},{8,0},{16,8},{24,16},{32,24},{40,32},{48,40},{56,48},{1,57}... | collective-permute-start | bytes 786440 | tf_op jit(solution)/shard_map/ppermute | solution.py:25
  33.8 7.9 %collective-permute-start.4 = (bf16[4,128,256]{2,1,0:T(8,128)(2,1)S(1)}, bf16[4,128,256]{2,1,0:T(8,128)(2,1)S(1)}, u32[]{:S(2)}, u32[]{:S(2)}) collective-permute-start(bf16[4,128,256]{2,1,0:T(8,128)(2,1)S(1)} %collective-permute-done.3.refs_6_), channel_id=1, source_target_pairs={{0,8},{8,16},{16,24},{24,32},{32,40},{40,48},{48,56},{56,0},{1,9},... | collective-permute-start | bytes 786440 | tf_op jit(solution)/shard_map/ppermute | solution.py:25
  49.3 8.9 %collective-permute-start.6 = (bf16[4,4,2,64,512]{4,3,2,1,0:T(8,128)(2,1)S(1)}, bf16[4,4,2,64,512]{4,3,2,1,0:T(8,128)(2,1)}, u32[]{:S(2)}, u32[]{:S(2)}) collective-permute-start(bf16[4,4,2,64,512]{4,3,2,1,0:T(8,128)(2,1)S(1)} %bitcast.96), channel_id=1, source_target_pairs={{0,1},{1,0},{2,3},{3,2},{4,5},{5,4},{6,7},{7,6},{8,9},{9,8},{10,11... | collective-permute-start | bytes 6291464 | tf_op jit(solution)/shard_map/ppermute | solution.py:21
  50.3 8.0 %collective-permute-start.7 = (bf16[2,128,256]{2,1,0:T(8,128)(2,1)}, bf16[2,128,256]{2,1,0:T(8,128)(2,1)S(1)}, u32[]{:S(2)}, u32[]{:S(2)}) collective-permute-start(bf16[2,128,256]{2,1,0:T(8,128)(2,1)} %slice.141), channel_id=1, source_target_pairs={{0,8},{8,16},{16,24},{24,32},{32,40},{40,48},{48,56},{56,0},{1,9},... | collective-permute-start | bytes 393224 | tf_op jit(solution)/shard_map/ppermute | solution.py:25
  66.7 9.3 %collective-permute-start.11 = (bf16[128,512]{1,0:T(8,128)(2,1)S(1)}, bf16[128,512]{1,0:T(8,128)(2,1)S(1)}, u32[]{:S(2)}, u32[]{:S(2)}) collective-permute-start(bf16[128,512]{1,0:T(8,128)(2,1)S(1)} %slice.144.refs_1_), channel_id=1, source_target_pairs={{0,56},{8,0},{16,8},{24,16},{32,24},{40,32},{48,40},{56,48},{1,57}... | collective-permute-start | bytes 393224 | tf_op jit(solution)/shard_map/ppermute | solution.py:25
  74.0 7.8 %collective-permute-start.17 = (bf16[144,512]{1,0:T(8,128)(2,1)S(1)}, bf16[144,512]{1,0:T(8,128)(2,1)S(1)}, u32[]{:S(2)}, u32[]{:S(2)}) collective-permute-start(bf16[144,512]{1,0:T(8,128)(2,1)S(1)} %collective-permute-done.16.refs_14_), channel_id=1, source_target_pairs={{0,8},{8,16},{16,24},{24,32},{32,40},{40,48},{48,56},{56,0},{1,9},... | collective-permute-start | bytes 442376 | tf_op jit(solution)/shard_map/ppermute | solution.py:25
  74.0 9.6 %collective-permute-start.21 = (bf16[128,512]{1,0:T(8,128)(2,1)S(1)}, bf16[128,512]{1,0:T(8,128)(2,1)S(1)}, u32[]{:S(2)}, u32[]{:S(2)}) collective-permute-start(bf16[128,512]{1,0:T(8,128)(2,1)S(1)} %slice.144.refs_1_), channel_id=1, source_target_pairs={{0,8},{8,16},{16,24},{24,32},{32,40},{40,48},{48,56},{56,0},{1,9},... | collective-permute-start | bytes 393224 | tf_op jit(solution)/shard_map/ppermute | solution.py:25
  77.6 12.4 %collective-permute-start.12 = (bf16[144,512]{1,0:T(8,128)(2,1)S(1)}, bf16[144,512]{1,0:T(8,128)(2,1)S(1)}, u32[]{:S(2)}, u32[]{:S(2)}) collective-permute-start(bf16[144,512]{1,0:T(8,128)(2,1)S(1)} %collective-permute-done.10.refs_2_), channel_id=1, source_target_pairs={{0,56},{8,0},{16,8},{24,16},{32,24},{40,32},{48,40},{56,48},{1,57}... | collective-permute-start | bytes 442376 | tf_op jit(solution)/shard_map/ppermute | solution.py:25
  81.8 11.6 %collective-permute-start.18 = (bf16[144,512]{1,0:T(8,128)(2,1)S(1)}, bf16[144,512]{1,0:T(8,128)(2,1)S(1)}, u32[]{:S(2)}, u32[]{:S(2)}) collective-permute-start(bf16[144,512]{1,0:T(8,128)(2,1)S(1)} %collective-permute-done.17.refs_12_), channel_id=1, source_target_pairs={{0,8},{8,16},{16,24},{24,32},{32,40},{40,48},{48,56},{56,0},{1,9},... | collective-permute-start | bytes 442376 | tf_op jit(solution)/shard_map/ppermute | solution.py:25
  83.6 9.7 %collective-permute-start.15 = (bf16[128,512]{1,0:T(8,128)(2,1)S(1)}, bf16[128,512]{1,0:T(8,128)(2,1)S(1)}, u32[]{:S(2)}, u32[]{:S(2)}) collective-permute-start(bf16[128,512]{1,0:T(8,128)(2,1)S(1)} %collective-permute-done.13.refs_5_), channel_id=1, source_target_pairs={{0,56},{8,0},{16,8},{24,16},{32,24},{40,32},{48,40},{56,48},{1,57}... | collective-permute-start | bytes 393224 | tf_op jit(solution)/shard_map/ppermute | solution.py:25
  86.9 25.4 %collective-permute-start.25 = (bf16[4,512,256]{2,1,0:T(8,128)(2,1)}, bf16[4,512,256]{2,1,0:T(8,128)(2,1)S(1)}, u32[]{:S(2)}, u32[]{:S(2)}) collective-permute-start(bf16[4,512,256]{2,1,0:T(8,128)(2,1)} %get-tuple-element.48), channel_id=1, source_target_pairs={{0,1},{1,0},{2,3},{3,2},{4,5},{5,4},{6,7},{7,6},{8,9},{9,8},{10,11... | collective-permute-start | bytes 3145736 | tf_op jit(solution)/shard_map/ppermute | solution.py:21
  90.1 8.4 %collective-permute-start.23 = (bf16[128,512]{1,0:T(8,128)(2,1)S(1)}, bf16[128,512]{1,0:T(8,128)(2,1)S(1)}, u32[]{:S(2)}, u32[]{:S(2)}) collective-permute-start(bf16[128,512]{1,0:T(8,128)(2,1)S(1)} %collective-permute-done.22.refs_13_), channel_id=1, source_target_pairs={{0,8},{8,16},{16,24},{24,32},{32,40},{40,48},{48,56},{56,0},{1,9},... | collective-permute-start | bytes 393224 | tf_op jit(solution)/shard_map/ppermute | solution.py:25
  90.1 8.4 %collective-permute-start.14 = (bf16[144,512]{1,0:T(8,128)(2,1)S(1)}, bf16[144,512]{1,0:T(8,128)(2,1)S(1)}, u32[]{:S(2)}, u32[]{:S(2)}) collective-permute-start(bf16[144,512]{1,0:T(8,128)(2,1)S(1)} %collective-permute-done.12.refs_4_), channel_id=1, source_target_pairs={{0,56},{8,0},{16,8},{24,16},{32,24},{40,32},{48,40},{56,48},{1,57}... | collective-permute-start | bytes 442376 | tf_op jit(solution)/shard_map/ppermute | solution.py:25
  104.3 20.8 %all-to-all-start.2 = ((bf16[16,16,2176]{2,1,0:T(8,128)(2,1)}), bf16[16,16,2176]{2,1,0:T(8,128)(2,1)S(1)}, u32[]{:S(2)}, u32[]{:S(2)}) async-start(bf16[16,16,2176]{2,1,0:T(8,128)(2,1)} %bitcast.105), calls=%async_computation.2 | async-start | bytes 2228224 | tf_op jit(solution)/shard_map/all_to_all | solution.py:29
  153.0 17.4 %collective-permute-start.29 = (bf16[272,256]{1,0:T(8,128)(2,1)}, bf16[272,256]{1,0:T(8,128)(2,1)S(1)}, u32[]{:S(2)}, u32[]{:S(2)}) collective-permute-start(bf16[272,256]{1,0:T(8,128)(2,1)} %get-tuple-element.59), channel_id=1, source_target_pairs={{0,56},{8,0},{16,8},{24,16},{32,24},{40,32},{48,40},{56,48},{1,57}... | collective-permute-start | bytes 417800 | tf_op jit(solution)/shard_map/ppermute | solution.py:25
  158.5 47.2 %all-to-all-start.4 = ((bf16[16,2,64,512]{3,2,1,0:T(8,128)(2,1)}), bf16[16,2,64,512]{3,2,1,0:T(8,128)(2,1)S(1)}, u32[]{:S(2)}, u32[]{:S(2)}) async-start(bf16[16,2,64,512]{3,2,1,0:T(8,128)(2,1)} %bitcast.99), calls=%async_computation.4 | async-start | bytes 4194304 | tf_op jit(solution)/shard_map/all_to_all | solution.py:29
  176.9 8.9 %collective-permute-start.30 = (bf16[528,256]{1,0:T(8,128)(2,1)S(1)}, bf16[528,256]{1,0:T(8,128)(2,1)S(1)}, u32[]{:S(2)}, u32[]{:S(2)}) collective-permute-start(bf16[528,256]{1,0:T(8,128)(2,1)S(1)} %get-tuple-element.81), channel_id=1, source_target_pairs={{0,8},{8,16},{16,24},{24,32},{32,40},{40,48},{48,56},{56,0},{1,9},... | collective-permute-start | bytes 811016 | tf_op jit(solution)/shard_map/ppermute | solution.py:25
  177.5 8.3 %collective-permute-start.31 = (bf16[528,256]{1,0:T(8,128)(2,1)S(1)}, bf16[528,256]{1,0:T(8,128)(2,1)S(1)}, u32[]{:S(2)}, u32[]{:S(2)}) collective-permute-start(bf16[528,256]{1,0:T(8,128)(2,1)S(1)} %get-tuple-element.80), channel_id=1, source_target_pairs={{0,56},{8,0},{16,8},{24,16},{32,24},{40,32},{48,40},{56,48},{1,57}... | collective-permute-start | bytes 811016 | tf_op jit(solution)/shard_map/ppermute | solution.py:25
  186.9 8.0 %collective-permute-start.32 = (bf16[528,256]{1,0:T(8,128)(2,1)S(1)}, bf16[528,256]{1,0:T(8,128)(2,1)S(1)}, u32[]{:S(2)}, u32[]{:S(2)}) collective-permute-start(bf16[528,256]{1,0:T(8,128)(2,1)S(1)} %get-tuple-element.79), channel_id=1, source_target_pairs={{0,8},{8,16},{16,24},{24,32},{32,40},{40,48},{48,56},{56,0},{1,9},... | collective-permute-start | bytes 811016 | tf_op jit(solution)/shard_map/ppermute | solution.py:25
  187.0 8.0 %collective-permute-start.33 = (bf16[528,256]{1,0:T(8,128)(2,1)S(1)}, bf16[528,256]{1,0:T(8,128)(2,1)S(1)}, u32[]{:S(2)}, u32[]{:S(2)}) collective-permute-start(bf16[528,256]{1,0:T(8,128)(2,1)S(1)} %get-tuple-element.78), channel_id=1, source_target_pairs={{0,56},{8,0},{16,8},{24,16},{32,24},{40,32},{48,40},{56,48},{1,57}... | collective-permute-start | bytes 811016 | tf_op jit(solution)/shard_map/ppermute | solution.py:25
  196.1 7.7 %collective-permute-start.34 = (bf16[528,256]{1,0:T(8,128)(2,1)S(1)}, bf16[528,256]{1,0:T(8,128)(2,1)S(1)}, u32[]{:S(2)}, u32[]{:S(2)}) collective-permute-start(bf16[528,256]{1,0:T(8,128)(2,1)S(1)} %get-tuple-element.76), channel_id=1, source_target_pairs={{0,8},{8,16},{16,24},{24,32},{32,40},{40,48},{48,56},{56,0},{1,9},... | collective-permute-start | bytes 811016 | tf_op jit(solution)/shard_map/ppermute | solution.py:25
  205.7 10.9 %all-to-all-start.5 = ((bf16[4,128,256]{2,1,0:T(8,128)(2,1)}), bf16[4,128,256]{2,1,0:T(8,128)(2,1)S(1)}, u32[]{:S(2)}, u32[]{:S(2)}) async-start(bf16[4,128,256]{2,1,0:T(8,128)(2,1)} %bitcast.30), calls=%async_computation.5 | async-start | bytes 524288 | tf_op jit(solution)/shard_map/all_to_all | solution.py:29
  (50 other events, 487.2 us)

commit v3 on v2

--- a/solution.py
+++ b/solution.py
@@ -65,7 +65,7 @@
             left = jnp.concatenate([high, left], axis=0)
         right = hop((terms[d].astype(F32) + right).astype(BF), 1)
         left = hop((terms[NZ - d].astype(F32) + left).astype(BF), -1)
-    return terms[0].astype(F32) + right.astype(F32) + left.astype(F32)
+    return terms[0], right, left
 
 
 def split3(v):
@@ -323,7 +323,8 @@
     )
     gram_half = exchange(copies(gram_rows, NX * NY), CHIPS).reshape(blk, NZ * blk)
     squares = gram_half.astype(F32)
-    share = (share + jnp.sum(squares * squares) / ((total_rows - 1.0) ** 2 * full_width)).reshape(1, 1)
+    squares = jnp.sum(squares * squares)
+    share = (share + squares / ((total_rows - 1.0) ** 2 * full_width)).reshape(1, 1)
     spread_view = dot(gram_half, gathered, 1, 0)
     spread_own = spread_view[:, :sub]
     spread_back = swap_core(spread_view[:, sub:])
@@ -386,9 +387,9 @@
         name="weight_terms",
     )(place, h_own, h_oth, later, share)
 
-    weight_sum = ring_sum(weight_part, right, left)
-    loss_rows = weight_sum[NX * kz :]
-    weight_sum = weight_sum[: NX * kz].astype(BF).reshape(NX, kz, sub)
+    arrived = ring_sum(weight_part, right, left)
+    loss_rows = sum(v[NX * kz :].astype(F32) for v in arrived)
+    weight_sum = sum(v[: NX * kz].astype(F32) for v in arrived).astype(BF).reshape(NX, kz, sub)
     weight_sum, loss_rows, input_parts = lax.optimization_barrier((weight_sum, loss_rows, input_parts))
     loss_part = jnp.sum(loss_rows).reshape(1, 1)
     blocks = exchange(weight_sum, "x")

time: 220 us -> 221 us (level)
  transfers between devices with their start and end apart: 42 -> 42, of which waited for: 22 -> 22; matrix products, arithmetic and copies ran while one was open for 7% -> 7% of each run, Pallas kernels for 10% -> 6%
where the time goes in v3:
time: 221 us; the launch traced here: 220 us
  starting transfers between devices  75.2 us (34%)
  waiting for transfers between devices  67.7 us (31%)
  Pallas kernels  28.7 us (13%)
  blocking collectives  18.6 us (8%)
  other arithmetic  14.4 us (7%)
  local copies, waits for them, and re-layouts  8.85 us (4%)
  between operations  5.43 us (2%)
    ppermute x30, waiting for transfers between devices, hop(): return lax.ppermute(v, 'z', [(i, (i + k) % NZ) for i in range(NZ)])  49 us
    ppermute x30, starting transfers between devices, hop(): return lax.ppermute(v, 'z', [(i, (i + k) % NZ) for i in range(NZ)])  48.6 us
    all_to_all x5, starting transfers between devices, exchange(): return lax.all_to_all(v, axes, split_axis=0, concat_axis=0, tiled=True)  25.8 us
    all_to_all x1, blocking collectives, exchange(): return lax.all_to_all(v, axes, split_axis=0, concat_axis=0, tiled=True)  18.6 us
    all_to_all x5, waiting for transfers between devices, exchange(): return lax.all_to_all(v, axes, split_axis=0, concat_axis=0, tiled=True)  15.2 us
    pallas_call x1, Pallas kernels, on_device(): pl.pallas_call(views_kernel, grid=(NY,), in_specs=[smem, at_dim(hblock, 1...  5.96 us
    pallas_call x1, Pallas kernels, on_device(): pl.pallas_call(turn_kernel, grid=(NY,), in_specs=[at_dim(hblock, 1), at_d...  5.86 us
    pallas_call x1, Pallas kernels, on_device(): pl.pallas_call(weight_kernel, grid=(NY,), in_specs=[smem] + [at_dim((1, k...  5.37 us
  transfers between devices with their start and end apart: 42, of which 22 were waited for; matrix products, arithmetic and copies ran while one was open for 7% of the time, Pallas kernels for 6%

profile of v3, /device:TPU:8, one launch (start us, length us, event | category | flops | bytes accessed | tf_op | source)
XLA Modules:
  0.0 219.5 jit_solution(3671211582978408018)
XLA Ops:
  2.3 4.3 %all-to-all-start = ((bf16[4,128,256]{2,1,0:T(8,128)(2,1)}), bf16[4,128,256]{2,1,0:T(8,128)(2,1)S(1)}, u32[]{:S(2)}, u32[]{:S(2)}) async-start(bf16[4,128,256]{2,1,0:T(8,128)(2,1)} %pad_maximum_fusion), calls=%async_computation | async-start | bytes 524288 | tf_op jit(solution)/shard_map/all_to_all | solution.py:29
  7.5 5.8 %all-to-all-done.refs_0_ = bf16[4,128,256]{2,1,0:T(8,128)(2,1)S(1)} async-done(((bf16[4,128,256]{2,1,0:T(8,128)(2,1)}), bf16[4,128,256]{2,1,0:T(8,128)(2,1)S(1)}, u32[]{:S(2)}, u32[]{:S(2)}) %all-to-all-start) | async-done | bytes 262176 | tf_op jit(solution)/shard_map/all_to_all | solution.py:29
  14.9 5.5 %all-to-all-start.1 = ((bf16[16,2,64,512]{3,2,1,0:T(8,128)(2,1)}), bf16[16,2,64,512]{3,2,1,0:T(8,128)(2,1)S(1)}, u32[]{:S(2)}, u32[]{:S(2)}) async-start(bf16[16,2,64,512]{3,2,1,0:T(8,128)(2,1)} %broadcast_in_dim.4), calls=%async_computation.1 | async-start | bytes 4194304 | tf_op jit(solution)/shard_map/all_to_all | solution.py:29
  20.4 5.9 %collective-permute-start = (bf16[4,128,256]{2,1,0:T(8,128)(2,1)S(1)}, bf16[4,128,256]{2,1,0:T(8,128)(2,1)S(1)}, u32[]{:S(2)}, u32[]{:S(2)}) collective-permute-start(bf16[4,128,256]{2,1,0:T(8,128)(2,1)S(1)} %all-to-all-done.refs_0_), channel_id=1, source_target_pairs={{0,56},{8,0},{16,8},{24,16},{32,24},{40,32},{48,40},{56,48},{1,57}... | collective-permute-start | bytes 786440 | tf_op jit(solution)/shard_map/ppermute | solution.py:25
  26.3 3.9 %collective-permute-done.refs_1_ = bf16[4,128,256]{2,1,0:T(8,128)(2,1)S(1)} collective-permute-done((bf16[4,128,256]{2,1,0:T(8,128)(2,1)S(1)}, bf16[4,128,256]{2,1,0:T(8,128)(2,1)S(1)}, u32[]{:S(2)}, u32[]{:S(2)}) %collective-permute-start) | collective-permute-done | bytes 262176 | tf_op jit(solution)/shard_map/ppermute | solution.py:25
  30.1 3.7 %collective-permute-start.1 = (bf16[4,128,256]{2,1,0:T(8,128)(2,1)S(1)}, bf16[4,128,256]{2,1,0:T(8,128)(2,1)S(1)}, u32[]{:S(2)}, u32[]{:S(2)}) collective-permute-start(bf16[4,128,256]{2,1,0:T(8,128)(2,1)S(1)} %collective-permute-done.refs_1_), channel_id=1, source_target_pairs={{0,56},{8,0},{16,8},{24,16},{32,24},{40,32},{48,40},{56,48},{1,57}... | collective-permute-start | bytes 786440 | tf_op jit(solution)/shard_map/ppermute | solution.py:25
  33.8 3.9 %collective-permute-done.1.refs_2_ = bf16[4,128,256]{2,1,0:T(8,128)(2,1)S(1)} collective-permute-done((bf16[4,128,256]{2,1,0:T(8,128)(2,1)S(1)}, bf16[4,128,256]{2,1,0:T(8,128)(2,1)S(1)}, u32[]{:S(2)}, u32[]{:S(2)}) %collective-permute-start.1) | collective-permute-done | bytes 262176 | tf_op jit(solution)/shard_map/ppermute | solution.py:25
  37.7 3.7 %collective-permute-start.2 = (bf16[4,128,256]{2,1,0:T(8,128)(2,1)S(1)}, bf16[4,128,256]{2,1,0:T(8,128)(2,1)S(1)}, u32[]{:S(2)}, u32[]{:S(2)}) collective-permute-start(bf16[4,128,256]{2,1,0:T(8,128)(2,1)S(1)} %collective-permute-done.1.refs_2_), channel_id=1, source_target_pairs={{0,56},{8,0},{16,8},{24,16},{32,24},{40,32},{48,40},{56,48},{1,57}... | collective-permute-start | bytes 786440 | tf_op jit(solution)/shard_map/ppermute | solution.py:25
  45.4 4.0 %collective-permute-done.5.refs_4_ = bf16[4,128,256]{2,1,0:T(8,128)(2,1)S(1)} collective-permute-done((bf16[4,128,256]{2,1,0:T(8,128)(2,1)S(1)}, bf16[4,128,256]{2,1,0:T(8,128)(2,1)S(1)}, u32[]{:S(2)}, u32[]{:S(2)}) %collective-permute-start.5) | collective-permute-done | bytes 262176 | tf_op jit(solution)/shard_map/ppermute | solution.py:25
  50.9 3.7 %collective-permute-start.8 = (bf16[2,128,256]{2,1,0:T(8,128)(2,1)}, bf16[2,128,256]{2,1,0:T(8,128)(2,1)}, u32[]{:S(2)}, u32[]{:S(2)}) collective-permute-start(bf16[2,128,256]{2,1,0:T(8,128)(2,1)} %slice.158), channel_id=1, source_target_pairs={{0,56},{8,0},{16,8},{24,16},{32,24},{40,32},{48,40},{56,48},{1,57}... | collective-permute-start | bytes 393224 | tf_op jit(solution)/shard_map/ppermute | solution.py:25
  58.9 6.0 %views.1 = (bf16[4,512,256]{2,1,0:T(8,128)(2,1)}, bf16[4,512,256]{2,1,0:T(8,128)(2,1)}, f32[2,256,256]{2,1,0:T(8,128)}, bf16[272,256]{1,0:T(8,128)(2,1)}, bf16[272,256]{1,0:T(8,128)(2,1)}, /*index=5*/f32[8,256]{1,0:T(8,128)}) custom-call(s32[2]{0:T(128)} %pad_add_fusion.place_ref, bf16[4,4,2,64,512]{4,3,2,1,0:T(8,128)(2,1)} %bitcast.102, ...), custom_call_target="tpu_custom_call" | custom-call | tf_op jit(solution)/shard_map/views/pallas_call | solution.py:249
  100.4 3.9 %gram.1 = (bf16[2048,512]{1,0:T(8,128)(2,1)}, bf16[256,2176]{1,0:T(8,128)(2,1)}, f32[8,512]{1,0:T(8,128)}) custom-call(f32[1,1]{1,0:T(1,128)} %bitcast.11.diff_ref, bf16[144,512]{1,0:T(8,128)(2,1)} %copy-done.5, bf16[128,512]{1,0:T(8,128)(2,1)} %copy-done.8, bf16[144,512]{1,0:T(8,128)(2,1)} %copy-done.15, bf16[128,512]{1,0:T(8,128)(2,1)} %copy-done.21, ...), custom_call_target="tpu_custom_call" | custom-call | tf_op jit(solution)/shard_map/gram/pallas_call | solution.py:288
  104.3 6.7 %all-to-all-start.2 = ((bf16[16,16,2176]{2,1,0:T(8,128)(2,1)}), bf16[16,16,2176]{2,1,0:T(8,128)(2,1)S(1)}, u32[]{:S(2)}, u32[]{:S(2)}) async-start(bf16[16,16,2176]{2,1,0:T(8,128)(2,1)} %bitcast.110), calls=%async_computation.2 | async-start | bytes 2228224 | tf_op jit(solution)/shard_map/all_to_all | solution.py:29
  113.3 5.9 %turn.1 = (bf16[4,512,512]{2,1,0:T(8,128)(2,1)}, bf16[4,512,512]{2,1,0:T(8,128)(2,1)}, bf16[4,512,512]{2,1,0:T(8,128)(2,1)}) custom-call(bf16[4,4,2,64,512]{4,3,2,1,0:T(8,128)(2,1)} %bitcast.103, bf16[4,4,2,64,512]{4,3,2,1,0:T(8,128)(2,1)} %collective-permute-done.6.oth_ref, bf16[4,512,256]{2,1,0:T(8,128)(2,1)} %get-tuple-element.47.kept_ref, ...), custom_call_target="tpu_custom_call" | custom-call | tf_op jit(solution)/shard_map/turn/pallas_call | solution.py:311
  119.2 6.0 %all-to-all-done.2 = bf16[16,16,2176]{2,1,0:T(8,128)(2,1)S(1)} async-done(((bf16[16,16,2176]{2,1,0:T(8,128)(2,1)}), bf16[16,16,2176]{2,1,0:T(8,128)(2,1)S(1)}, u32[]{:S(2)}, u32[]{:S(2)}) %all-to-all-start.2) | async-done | bytes 1114144 | tf_op jit(solution)/shard_map/all_to_all | solution.py:29
  126.0 18.6 %all_to_all.30 = bf16[16,16,2048]{2,1,0:T(8,128)(2,1)S(1)} all-to-all(bf16[16,16,2048]{2,1,0:T(8,128)(2,1)S(1)} %broadcast_in_dim.5), channel_id=1, replica_groups=mesh['x'=4,'z'=8,'y'=4,'c'=2] {'x','y'}, dimensions={0} | all-to-all | bytes 2097152 | tf_op jit(solution)/shard_map/all_to_all | solution.py:29
  155.1 5.2 %collective-permute-done.28 = bf16[256,256]{1,0:T(8,128)(2,1)S(1)} collective-permute-done((bf16[256,256]{1,0:T(8,128)(2,1)}, bf16[256,256]{1,0:T(8,128)(2,1)S(1)}, u32[]{:S(2)}, u32[]{:S(2)}) %collective-permute-start.28) | collective-permute-done | bytes 131104 | tf_op jit(solution)/shard_map/ppermute | solution.py:25
  161.0 4.7 %input_terms.1 = bf16[4,512,512]{2,1,0:T(8,128)(2,1)} custom-call(bf16[512,256]{1,0:T(8,128)(2,1)} %bitcast.107, bf16[512,256]{1,0:T(8,128)(2,1)} %copy-done.13, bf16[4,512,512]{2,1,0:T(8,128)(2,1)} %get-tuple-element.61.w_ref), custom_call_target="tpu_custom_call" | custom-call | tf_op jit(solution)/shard_map/input_terms/pallas_call | solution.py:369
  165.7 5.4 %weight_terms.1 = bf16[8,528,256]{2,1,0:T(8,128)(2,1)} custom-call(s32[2]{0:T(128)} %pad_add_fusion.place_ref, bf16[4,512,512]{2,1,0:T(8,128)(2,1)} %get-tuple-element.52.own_ref, bf16[4,512,512]{2,1,0:T(8,128)(2,1)} %get-tuple-element.53.oth_ref, bf16[512,256]{1,0:T(8,128)(2,1)} %bitcast.108, f32[1,1]{1,0:T(1,128)} %bitcast.22.share_ref), custom_call_target="tpu_custom_call" | custom-call | tf_op jit(solution)/shard_map/weight_terms/pallas_call | solution.py:381
  171.1 5.0 %all-to-all-start.4 = ((bf16[16,2,64,512]{3,2,1,0:T(8,128)(2,1)}), bf16[16,2,64,512]{3,2,1,0:T(8,128)(2,1)S(1)}, u32[]{:S(2)}, u32[]{:S(2)}) async-start(bf16[16,2,64,512]{3,2,1,0:T(8,128)(2,1)} %bitcast.104), calls=%async_computation.4 | async-start | bytes 4194304 | tf_op jit(solution)/shard_map/all_to_all | solution.py:29
  180.5 5.6 %collective-permute-done.30 = bf16[528,256]{1,0:T(8,128)(2,1)S(1)} collective-permute-done((bf16[528,256]{1,0:T(8,128)(2,1)S(1)}, bf16[528,256]{1,0:T(8,128)(2,1)S(1)}, u32[]{:S(2)}, u32[]{:S(2)}) %collective-permute-start.30) | collective-permute-done | bytes 270368 | tf_op jit(solution)/shard_map/ppermute | solution.py:25
  190.6 4.7 %collective-permute-done.32 = bf16[528,256]{1,0:T(8,128)(2,1)S(1)} collective-permute-done((bf16[528,256]{1,0:T(8,128)(2,1)S(1)}, bf16[528,256]{1,0:T(8,128)(2,1)S(1)}, u32[]{:S(2)}, u32[]{:S(2)}) %collective-permute-start.32) | collective-permute-done | bytes 270368 | tf_op jit(solution)/shard_map/ppermute | solution.py:25
  199.8 4.4 %collective-permute-done.34 = bf16[528,256]{1,0:T(8,128)(2,1)S(1)} collective-permute-done((bf16[528,256]{1,0:T(8,128)(2,1)S(1)}, bf16[528,256]{1,0:T(8,128)(2,1)S(1)}, u32[]{:S(2)}, u32[]{:S(2)}) %collective-permute-start.34) | collective-permute-done | bytes 270368 | tf_op jit(solution)/shard_map/ppermute | solution.py:25
  206.7 4.3 %all-to-all-start.5 = ((bf16[4,128,256]{2,1,0:T(8,128)(2,1)}), bf16[4,128,256]{2,1,0:T(8,128)(2,1)S(1)}, u32[]{:S(2)}, u32[]{:S(2)}) async-start(bf16[4,128,256]{2,1,0:T(8,128)(2,1)} %bitcast.30), calls=%async_computation.5 | async-start | bytes 524288 | tf_op jit(solution)/shard_map/all_to_all | solution.py:29
  (167 shorter events, 83.5 us)
Async XLA Ops:
  2.3 11.0 %all-to-all-start = ((bf16[4,128,256]{2,1,0:T(8,128)(2,1)}), bf16[4,128,256]{2,1,0:T(8,128)(2,1)S(1)}, u32[]{:S(2)}, u32[]{:S(2)}) async-start(bf16[4,128,256]{2,1,0:T(8,128)(2,1)} %pad_maximum_fusion), calls=%async_computation | async-start | bytes 524288 | tf_op jit(solution)/shard_map/all_to_all | solution.py:29
  14.9 34.5 %all-to-all-start.1 = ((bf16[16,2,64,512]{3,2,1,0:T(8,128)(2,1)}), bf16[16,2,64,512]{3,2,1,0:T(8,128)(2,1)S(1)}, u32[]{:S(2)}, u32[]{:S(2)}) async-start(bf16[16,2,64,512]{3,2,1,0:T(8,128)(2,1)} %broadcast_in_dim.4), calls=%async_computation.1 | async-start | bytes 4194304 | tf_op jit(solution)/shard_map/all_to_all | solution.py:29
  20.4 9.7 %collective-permute-start = (bf16[4,128,256]{2,1,0:T(8,128)(2,1)S(1)}, bf16[4,128,256]{2,1,0:T(8,128)(2,1)S(1)}, u32[]{:S(2)}, u32[]{:S(2)}) collective-permute-start(bf16[4,128,256]{2,1,0:T(8,128)(2,1)S(1)} %all-to-all-done.refs_0_), channel_id=1, source_target_pairs={{0,56},{8,0},{16,8},{24,16},{32,24},{40,32},{48,40},{56,48},{1,57}... | collective-permute-start | bytes 786440 | tf_op jit(solution)/shard_map/ppermute | solution.py:25
  33.8 7.9 %collective-permute-start.4 = (bf16[4,128,256]{2,1,0:T(8,128)(2,1)S(1)}, bf16[4,128,256]{2,1,0:T(8,128)(2,1)S(1)}, u32[]{:S(2)}, u32[]{:S(2)}) collective-permute-start(bf16[4,128,256]{2,1,0:T(8,128)(2,1)S(1)} %collective-permute-done.3.refs_6_), channel_id=1, source_target_pairs={{0,8},{8,16},{16,24},{24,32},{32,40},{40,48},{48,56},{56,0},{1,9},... | collective-permute-start | bytes 786440 | tf_op jit(solution)/shard_map/ppermute | solution.py:25
  49.3 8.9 %collective-permute-start.6 = (bf16[4,4,2,64,512]{4,3,2,1,0:T(8,128)(2,1)S(1)}, bf16[4,4,2,64,512]{4,3,2,1,0:T(8,128)(2,1)}, u32[]{:S(2)}, u32[]{:S(2)}) collective-permute-start(bf16[4,4,2,64,512]{4,3,2,1,0:T(8,128)(2,1)S(1)} %bitcast.101), channel_id=1, source_target_pairs={{0,1},{1,0},{2,3},{3,2},{4,5},{5,4},{6,7},{7,6},{8,9},{9,8},{10,11... | collective-permute-start | bytes 6291464 | tf_op jit(solution)/shard_map/ppermute | solution.py:21
  50.3 8.0 %collective-permute-start.7 = (bf16[2,128,256]{2,1,0:T(8,128)(2,1)}, bf16[2,128,256]{2,1,0:T(8,128)(2,1)S(1)}, u32[]{:S(2)}, u32[]{:S(2)}) collective-permute-start(bf16[2,128,256]{2,1,0:T(8,128)(2,1)} %slice.157), channel_id=1, source_target_pairs={{0,8},{8,16},{16,24},{24,32},{32,40},{40,48},{48,56},{56,0},{1,9},... | collective-permute-start | bytes 393224 | tf_op jit(solution)/shard_map/ppermute | solution.py:25
  66.7 9.3 %collective-permute-start.11 = (bf16[128,512]{1,0:T(8,128)(2,1)S(1)}, bf16[128,512]{1,0:T(8,128)(2,1)S(1)}, u32[]{:S(2)}, u32[]{:S(2)}) collective-permute-start(bf16[128,512]{1,0:T(8,128)(2,1)S(1)} %slice.160.refs_1_), channel_id=1, source_target_pairs={{0,56},{8,0},{16,8},{24,16},{32,24},{40,32},{48,40},{56,48},{1,57}... | collective-permute-start | bytes 393224 | tf_op jit(solution)/shard_map/ppermute | solution.py:25
  74.0 7.9 %collective-permute-start.17 = (bf16[144,512]{1,0:T(8,128)(2,1)S(1)}, bf16[144,512]{1,0:T(8,128)(2,1)S(1)}, u32[]{:S(2)}, u32[]{:S(2)}) collective-permute-start(bf16[144,512]{1,0:T(8,128)(2,1)S(1)} %collective-permute-done.16.refs_14_), channel_id=1, source_target_pairs={{0,8},{8,16},{16,24},{24,32},{32,40},{40,48},{48,56},{56,0},{1,9},... | collective-permute-start | bytes 442376 | tf_op jit(solution)/shard_map/ppermute | solution.py:25
  74.0 9.6 %collective-permute-start.21 = (bf16[128,512]{1,0:T(8,128)(2,1)S(1)}, bf16[128,512]{1,0:T(8,128)(2,1)S(1)}, u32[]{:S(2)}, u32[]{:S(2)}) collective-permute-start(bf16[128,512]{1,0:T(8,128)(2,1)S(1)} %slice.160.refs_1_), channel_id=1, source_target_pairs={{0,8},{8,16},{16,24},{24,32},{32,40},{40,48},{48,56},{56,0},{1,9},... | collective-permute-start | bytes 393224 | tf_op jit(solution)/shard_map/ppermute | solution.py:25
  77.6 12.5 %collective-permute-start.12 = (bf16[144,512]{1,0:T(8,128)(2,1)S(1)}, bf16[144,512]{1,0:T(8,128)(2,1)S(1)}, u32[]{:S(2)}, u32[]{:S(2)}) collective-permute-start(bf16[144,512]{1,0:T(8,128)(2,1)S(1)} %collective-permute-done.10.refs_2_), channel_id=1, source_target_pairs={{0,56},{8,0},{16,8},{24,16},{32,24},{40,32},{48,40},{56,48},{1,57}... | collective-permute-start | bytes 442376 | tf_op jit(solution)/shard_map/ppermute | solution.py:25
  81.8 11.6 %collective-permute-start.18 = (bf16[144,512]{1,0:T(8,128)(2,1)S(1)}, bf16[144,512]{1,0:T(8,128)(2,1)S(1)}, u32[]{:S(2)}, u32[]{:S(2)}) collective-permute-start(bf16[144,512]{1,0:T(8,128)(2,1)S(1)} %collective-permute-done.17.refs_12_), channel_id=1, source_target_pairs={{0,8},{8,16},{16,24},{24,32},{32,40},{40,48},{48,56},{56,0},{1,9},... | collective-permute-start | bytes 442376 | tf_op jit(solution)/shard_map/ppermute | solution.py:25
  83.6 9.7 %collective-permute-start.15 = (bf16[128,512]{1,0:T(8,128)(2,1)S(1)}, bf16[128,512]{1,0:T(8,128)(2,1)S(1)}, u32[]{:S(2)}, u32[]{:S(2)}) collective-permute-start(bf16[128,512]{1,0:T(8,128)(2,1)S(1)} %collective-permute-done.13.refs_5_), channel_id=1, source_target_pairs={{0,56},{8,0},{16,8},{24,16},{32,24},{40,32},{48,40},{56,48},{1,57}... | collective-permute-start | bytes 393224 | tf_op jit(solution)/shard_map/ppermute | solution.py:25
  86.8 25.5 %collective-permute-start.25 = (bf16[4,512,256]{2,1,0:T(8,128)(2,1)}, bf16[4,512,256]{2,1,0:T(8,128)(2,1)S(1)}, u32[]{:S(2)}, u32[]{:S(2)}) collective-permute-start(bf16[4,512,256]{2,1,0:T(8,128)(2,1)} %get-tuple-element.48), channel_id=1, source_target_pairs={{0,1},{1,0},{2,3},{3,2},{4,5},{5,4},{6,7},{7,6},{8,9},{9,8},{10,11... | collective-permute-start | bytes 3145736 | tf_op jit(solution)/shard_map/ppermute | solution.py:21
  90.1 8.4 %collective-permute-start.23 = (bf16[128,512]{1,0:T(8,128)(2,1)S(1)}, bf16[128,512]{1,0:T(8,128)(2,1)S(1)}, u32[]{:S(2)}, u32[]{:S(2)}) collective-permute-start(bf16[128,512]{1,0:T(8,128)(2,1)S(1)} %collective-permute-done.22.refs_13_), channel_id=1, source_target_pairs={{0,8},{8,16},{16,24},{24,32},{32,40},{40,48},{48,56},{56,0},{1,9},... | collective-permute-start | bytes 393224 | tf_op jit(solution)/shard_map/ppermute | solution.py:25
  90.1 8.4 %collective-permute-start.14 = (bf16[144,512]{1,0:T(8,128)(2,1)S(1)}, bf16[144,512]{1,0:T(8,128)(2,1)S(1)}, u32[]{:S(2)}, u32[]{:S(2)}) collective-permute-start(bf16[144,512]{1,0:T(8,128)(2,1)S(1)} %collective-permute-done.12.refs_4_), channel_id=1, source_target_pairs={{0,56},{8,0},{16,8},{24,16},{32,24},{40,32},{48,40},{56,48},{1,57}... | collective-permute-start | bytes 442376 | tf_op jit(solution)/shard_map/ppermute | solution.py:25
  104.3 20.8 %all-to-all-start.2 = ((bf16[16,16,2176]{2,1,0:T(8,128)(2,1)}), bf16[16,16,2176]{2,1,0:T(8,128)(2,1)S(1)}, u32[]{:S(2)}, u32[]{:S(2)}) async-start(bf16[16,16,2176]{2,1,0:T(8,128)(2,1)} %bitcast.110), calls=%async_computation.2 | async-start | bytes 2228224 | tf_op jit(solution)/shard_map/all_to_all | solution.py:29
  147.2 13.0 %collective-permute-start.27 = (bf16[512,256]{1,0:T(8,128)(2,1)S(1)}, bf16[512,256]{1,0:T(8,128)(2,1)S(1)}, u32[]{:S(2)}, u32[]{:S(2)}) collective-permute-start(bf16[512,256]{1,0:T(8,128)(2,1)S(1)} %bitcast.105), channel_id=1, source_target_pairs={{0,1},{1,0},{2,3},{3,2},{4,5},{5,4},{6,7},{7,6},{8,9},{9,8},{10,11... | collective-permute-start | bytes 786440 | tf_op jit(solution)/shard_map/ppermute | solution.py:21
  171.1 35.6 %all-to-all-start.4 = ((bf16[16,2,64,512]{3,2,1,0:T(8,128)(2,1)}), bf16[16,2,64,512]{3,2,1,0:T(8,128)(2,1)S(1)}, u32[]{:S(2)}, u32[]{:S(2)}) async-start(bf16[16,2,64,512]{3,2,1,0:T(8,128)(2,1)} %bitcast.104), calls=%async_computation.4 | async-start | bytes 4194304 | tf_op jit(solution)/shard_map/all_to_all | solution.py:29
  177.2 8.9 %collective-permute-start.30 = (bf16[528,256]{1,0:T(8,128)(2,1)S(1)}, bf16[528,256]{1,0:T(8,128)(2,1)S(1)}, u32[]{:S(2)}, u32[]{:S(2)}) collective-permute-start(bf16[528,256]{1,0:T(8,128)(2,1)S(1)} %get-tuple-element.81), channel_id=1, source_target_pairs={{0,8},{8,16},{16,24},{24,32},{32,40},{40,48},{48,56},{56,0},{1,9},... | collective-permute-start | bytes 811016 | tf_op jit(solution)/shard_map/ppermute | solution.py:25
  177.8 8.3 %collective-permute-start.31 = (bf16[528,256]{1,0:T(8,128)(2,1)S(1)}, bf16[528,256]{1,0:T(8,128)(2,1)S(1)}, u32[]{:S(2)}, u32[]{:S(2)}) collective-permute-start(bf16[528,256]{1,0:T(8,128)(2,1)S(1)} %get-tuple-element.80), channel_id=1, source_target_pairs={{0,56},{8,0},{16,8},{24,16},{32,24},{40,32},{48,40},{56,48},{1,57}... | collective-permute-start | bytes 811016 | tf_op jit(solution)/shard_map/ppermute | solution.py:25
  187.3 8.1 %collective-permute-start.32 = (bf16[528,256]{1,0:T(8,128)(2,1)S(1)}, bf16[528,256]{1,0:T(8,128)(2,1)S(1)}, u32[]{:S(2)}, u32[]{:S(2)}) collective-permute-start(bf16[528,256]{1,0:T(8,128)(2,1)S(1)} %get-tuple-element.79), channel_id=1, source_target_pairs={{0,8},{8,16},{16,24},{24,32},{32,40},{40,48},{48,56},{56,0},{1,9},... | collective-permute-start | bytes 811016 | tf_op jit(solution)/shard_map/ppermute | solution.py:25
  187.4 8.0 %collective-permute-start.33 = (bf16[528,256]{1,0:T(8,128)(2,1)S(1)}, bf16[528,256]{1,0:T(8,128)(2,1)S(1)}, u32[]{:S(2)}, u32[]{:S(2)}) collective-permute-start(bf16[528,256]{1,0:T(8,128)(2,1)S(1)} %get-tuple-element.78), channel_id=1, source_target_pairs={{0,56},{8,0},{16,8},{24,16},{32,24},{40,32},{48,40},{56,48},{1,57}... | collective-permute-start | bytes 811016 | tf_op jit(solution)/shard_map/ppermute | solution.py:25
  196.5 7.7 %collective-permute-start.34 = (bf16[528,256]{1,0:T(8,128)(2,1)S(1)}, bf16[528,256]{1,0:T(8,128)(2,1)S(1)}, u32[]{:S(2)}, u32[]{:S(2)}) collective-permute-start(bf16[528,256]{1,0:T(8,128)(2,1)S(1)} %get-tuple-element.76), channel_id=1, source_target_pairs={{0,8},{8,16},{16,24},{24,32},{32,40},{40,48},{48,56},{56,0},{1,9},... | collective-permute-start | bytes 811016 | tf_op jit(solution)/shard_map/ppermute | solution.py:25
  206.7 10.9 %all-to-all-start.5 = ((bf16[4,128,256]{2,1,0:T(8,128)(2,1)}), bf16[4,128,256]{2,1,0:T(8,128)(2,1)S(1)}, u32[]{:S(2)}, u32[]{:S(2)}) async-start(bf16[4,128,256]{2,1,0:T(8,128)(2,1)} %bitcast.30), calls=%async_computation.5 | async-start | bytes 524288 | tf_op jit(solution)/shard_map/all_to_all | solution.py:29
  (49 other events, 484.3 us)

commit v4 on v2

--- a/solution.py
+++ b/solution.py
@@ -15,6 +15,7 @@
 CHIPS = ("x", "y")
 SMEM = pltpu.SMEM
 STAT = 16
+PER = 2
 
 
 def swap_core(v):
@@ -187,10 +188,12 @@
     kz = own_ref.shape[1] // HALF
     rows = NY * kz
     for ref, lead in ((own_ref, core), (oth_ref, 1 - core)):
-        term = dot(ref[0], g_ref[...], 1, 0).astype(BF)
-        place = pl.ds(pl.multiple_of(step * kz, kz), kz)
-        for q in range(HALF):
-            out_ref[lax.rem(lead * HALF + q - zi + NZ, NZ), place] = term[q * kz : (q + 1) * kz]
+        term = dot(ref[...].reshape(-1, ref.shape[2]), g_ref[...], 1, 0).astype(BF)
+        for y in range(PER):
+            place = pl.ds(pl.multiple_of((step * PER + y) * kz, kz), kz)
+            for q in range(HALF):
+                lo = (y * HALF + q) * kz
+                out_ref[lax.rem(lead * HALF + q - zi + NZ, NZ), place] = term[lo : lo + kz]
 
     @pl.when(step == 0)
     def _():
@@ -379,8 +382,8 @@
     terms = NX * kz + STAT
     weight_part = pl.pallas_call(
         weight_kernel,
-        grid=(NY,),
-        in_specs=[smem] + [at_dim((1, kpart, flat), 0)] * 2 + [fixed((flat, sub)), fixed((1, 1))],
+        grid=(NY // PER,),
+        in_specs=[smem] + [at_dim((PER, kpart, flat), 0)] * 2 + [fixed((flat, sub)), fixed((1, 1))],
         out_specs=fixed((NZ, terms, sub)),
         out_shape=shape((NZ, terms, sub), BF),
         name="weight_terms",

time: 220 us -> 219 us (level)
  no operation moved by 1% of the time
where the time goes in v4:
time: 219 us; the launch traced here: 218 us
  starting transfers between devices  75.4 us (34%)
  waiting for transfers between devices  66.8 us (31%)
  Pallas kernels  27.9 us (13%)
  blocking collectives  18.6 us (8%)
  other arithmetic  13.1 us (6%)
  local copies, waits for them, and re-layouts  9.62 us (4%)
  between operations  5.55 us (3%)
    ppermute x30, starting transfers between devices, hop(): return lax.ppermute(v, 'z', [(i, (i + k) % NZ) for i in range(NZ)])  48.7 us
    ppermute x30, waiting for transfers between devices, hop(): return lax.ppermute(v, 'z', [(i, (i + k) % NZ) for i in range(NZ)])  48.3 us
    all_to_all x5, starting transfers between devices, exchange(): return lax.all_to_all(v, axes, split_axis=0, concat_axis=0, tiled=True)  25.9 us
    all_to_all x1, blocking collectives, exchange(): return lax.all_to_all(v, axes, split_axis=0, concat_axis=0, tiled=True)  18.6 us
    all_to_all x5, waiting for transfers between devices, exchange(): return lax.all_to_all(v, axes, split_axis=0, concat_axis=0, tiled=True)  15.1 us
    pallas_call x1, Pallas kernels, on_device(): pl.pallas_call(views_kernel, grid=(NY,), in_specs=[smem, at_dim(hblock, 1...  5.98 us
    pallas_call x1, Pallas kernels, on_device(): pl.pallas_call(turn_kernel, grid=(NY,), in_specs=[at_dim(hblock, 1), at_d...  5.87 us
    pallas_call x1, Pallas kernels, on_device(): pl.pallas_call(input_kernel, grid=(NY,), in_specs=[fixed((flat, sub)), fi...  4.74 us
  transfers between devices with their start and end apart: 42, of which 22 were waited for; matrix products, arithmetic and copies ran while one was open for 7% of the time, Pallas kernels for 10%

profile of v4, /device:TPU:8, one launch (start us, length us, event | category | flops | bytes accessed | tf_op | source)
XLA Modules:
  0.0 217.7 jit_solution(2281529105225952269)
XLA Ops:
  2.3 4.3 %all-to-all-start = ((bf16[4,128,256]{2,1,0:T(8,128)(2,1)}), bf16[4,128,256]{2,1,0:T(8,128)(2,1)S(1)}, u32[]{:S(2)}, u32[]{:S(2)}) async-start(bf16[4,128,256]{2,1,0:T(8,128)(2,1)} %pad_maximum_fusion), calls=%async_computation | async-start | bytes 524288 | tf_op jit(solution)/shard_map/all_to_all | solution.py:30
  7.5 5.8 %all-to-all-done.refs_0_ = bf16[4,128,256]{2,1,0:T(8,128)(2,1)S(1)} async-done(((bf16[4,128,256]{2,1,0:T(8,128)(2,1)}), bf16[4,128,256]{2,1,0:T(8,128)(2,1)S(1)}, u32[]{:S(2)}, u32[]{:S(2)}) %all-to-all-start) | async-done | bytes 262176 | tf_op jit(solution)/shard_map/all_to_all | solution.py:30
  14.9 5.5 %all-to-all-start.1 = ((bf16[16,2,64,512]{3,2,1,0:T(8,128)(2,1)}), bf16[16,2,64,512]{3,2,1,0:T(8,128)(2,1)S(1)}, u32[]{:S(2)}, u32[]{:S(2)}) async-start(bf16[16,2,64,512]{3,2,1,0:T(8,128)(2,1)} %broadcast_in_dim.4), calls=%async_computation.1 | async-start | bytes 4194304 | tf_op jit(solution)/shard_map/all_to_all | solution.py:30
  20.4 5.9 %collective-permute-start = (bf16[4,128,256]{2,1,0:T(8,128)(2,1)S(1)}, bf16[4,128,256]{2,1,0:T(8,128)(2,1)S(1)}, u32[]{:S(2)}, u32[]{:S(2)}) collective-permute-start(bf16[4,128,256]{2,1,0:T(8,128)(2,1)S(1)} %all-to-all-done.refs_0_), channel_id=1, source_target_pairs={{0,56},{8,0},{16,8},{24,16},{32,24},{40,32},{48,40},{56,48},{1,57}... | collective-permute-start | bytes 786440 | tf_op jit(solution)/shard_map/ppermute | solution.py:26
  26.3 3.9 %collective-permute-done.refs_1_ = bf16[4,128,256]{2,1,0:T(8,128)(2,1)S(1)} collective-permute-done((bf16[4,128,256]{2,1,0:T(8,128)(2,1)S(1)}, bf16[4,128,256]{2,1,0:T(8,128)(2,1)S(1)}, u32[]{:S(2)}, u32[]{:S(2)}) %collective-permute-start) | collective-permute-done | bytes 262176 | tf_op jit(solution)/shard_map/ppermute | solution.py:26
  30.1 3.7 %collective-permute-start.1 = (bf16[4,128,256]{2,1,0:T(8,128)(2,1)S(1)}, bf16[4,128,256]{2,1,0:T(8,128)(2,1)S(1)}, u32[]{:S(2)}, u32[]{:S(2)}) collective-permute-start(bf16[4,128,256]{2,1,0:T(8,128)(2,1)S(1)} %collective-permute-done.refs_1_), channel_id=1, source_target_pairs={{0,56},{8,0},{16,8},{24,16},{32,24},{40,32},{48,40},{56,48},{1,57}... | collective-permute-start | bytes 786440 | tf_op jit(solution)/shard_map/ppermute | solution.py:26
  33.8 3.9 %collective-permute-done.1.refs_2_ = bf16[4,128,256]{2,1,0:T(8,128)(2,1)S(1)} collective-permute-done((bf16[4,128,256]{2,1,0:T(8,128)(2,1)S(1)}, bf16[4,128,256]{2,1,0:T(8,128)(2,1)S(1)}, u32[]{:S(2)}, u32[]{:S(2)}) %collective-permute-start.1) | collective-permute-done | bytes 262176 | tf_op jit(solution)/shard_map/ppermute | solution.py:26
  37.7 3.7 %collective-permute-start.2 = (bf16[4,128,256]{2,1,0:T(8,128)(2,1)S(1)}, bf16[4,128,256]{2,1,0:T(8,128)(2,1)S(1)}, u32[]{:S(2)}, u32[]{:S(2)}) collective-permute-start(bf16[4,128,256]{2,1,0:T(8,128)(2,1)S(1)} %collective-permute-done.1.refs_2_), channel_id=1, source_target_pairs={{0,56},{8,0},{16,8},{24,16},{32,24},{40,32},{48,40},{56,48},{1,57}... | collective-permute-start | bytes 786440 | tf_op jit(solution)/shard_map/ppermute | solution.py:26
  45.4 4.0 %collective-permute-done.5.refs_4_ = bf16[4,128,256]{2,1,0:T(8,128)(2,1)S(1)} collective-permute-done((bf16[4,128,256]{2,1,0:T(8,128)(2,1)S(1)}, bf16[4,128,256]{2,1,0:T(8,128)(2,1)S(1)}, u32[]{:S(2)}, u32[]{:S(2)}) %collective-permute-start.5) | collective-permute-done | bytes 262176 | tf_op jit(solution)/shard_map/ppermute | solution.py:26
  50.9 3.7 %collective-permute-start.8 = (bf16[2,128,256]{2,1,0:T(8,128)(2,1)}, bf16[2,128,256]{2,1,0:T(8,128)(2,1)}, u32[]{:S(2)}, u32[]{:S(2)}) collective-permute-start(bf16[2,128,256]{2,1,0:T(8,128)(2,1)} %slice.142), channel_id=1, source_target_pairs={{0,56},{8,0},{16,8},{24,16},{32,24},{40,32},{48,40},{56,48},{1,57}... | collective-permute-start | bytes 393224 | tf_op jit(solution)/shard_map/ppermute | solution.py:26
  58.9 6.0 %views.1 = (bf16[4,512,256]{2,1,0:T(8,128)(2,1)}, bf16[4,512,256]{2,1,0:T(8,128)(2,1)}, f32[2,256,256]{2,1,0:T(8,128)}, bf16[272,256]{1,0:T(8,128)(2,1)}, bf16[272,256]{1,0:T(8,128)(2,1)}, /*index=5*/f32[8,256]{1,0:T(8,128)}) custom-call(s32[2]{0:T(128)} %pad_add_fusion.place_ref, bf16[4,4,2,64,512]{4,3,2,1,0:T(8,128)(2,1)} %bitcast.97, ...), custom_call_target="tpu_custom_call" | custom-call | tf_op jit(solution)/shard_map/views/pallas_call | solution.py:252
  100.4 3.9 %gram.1 = (bf16[2048,512]{1,0:T(8,128)(2,1)}, bf16[256,2176]{1,0:T(8,128)(2,1)}, f32[8,512]{1,0:T(8,128)}) custom-call(f32[1,1]{1,0:T(1,128)} %bitcast.11.diff_ref, bf16[144,512]{1,0:T(8,128)(2,1)} %copy-done.5, bf16[128,512]{1,0:T(8,128)(2,1)} %copy-done.8, bf16[144,512]{1,0:T(8,128)(2,1)} %copy-done.15, bf16[128,512]{1,0:T(8,128)(2,1)} %copy-done.21, ...), custom_call_target="tpu_custom_call" | custom-call | tf_op jit(solution)/shard_map/gram/pallas_call | solution.py:291
  104.3 6.7 %all-to-all-start.2 = ((bf16[16,16,2176]{2,1,0:T(8,128)(2,1)}), bf16[16,16,2176]{2,1,0:T(8,128)(2,1)S(1)}, u32[]{:S(2)}, u32[]{:S(2)}) async-start(bf16[16,16,2176]{2,1,0:T(8,128)(2,1)} %bitcast.105), calls=%async_computation.2 | async-start | bytes 2228224 | tf_op jit(solution)/shard_map/all_to_all | solution.py:30
  113.3 5.9 %turn.1 = (bf16[4,512,512]{2,1,0:T(8,128)(2,1)}, bf16[4,512,512]{2,1,0:T(8,128)(2,1)}, bf16[4,512,512]{2,1,0:T(8,128)(2,1)}) custom-call(bf16[4,4,2,64,512]{4,3,2,1,0:T(8,128)(2,1)} %bitcast.98, bf16[4,4,2,64,512]{4,3,2,1,0:T(8,128)(2,1)} %collective-permute-done.6.oth_ref, bf16[4,512,256]{2,1,0:T(8,128)(2,1)} %get-tuple-element.47.kept_ref, ...), custom_call_target="tpu_custom_call" | custom-call | tf_op jit(solution)/shard_map/turn/pallas_call | solution.py:314
  119.2 5.9 %all-to-all-done.2 = bf16[16,16,2176]{2,1,0:T(8,128)(2,1)S(1)} async-done(((bf16[16,16,2176]{2,1,0:T(8,128)(2,1)}), bf16[16,16,2176]{2,1,0:T(8,128)(2,1)S(1)}, u32[]{:S(2)}, u32[]{:S(2)}) %all-to-all-start.2) | async-done | bytes 1114144 | tf_op jit(solution)/shard_map/all_to_all | solution.py:30
  126.0 18.6 %all_to_all.30 = bf16[16,16,2048]{2,1,0:T(8,128)(2,1)S(1)} all-to-all(bf16[16,16,2048]{2,1,0:T(8,128)(2,1)S(1)} %broadcast_in_dim.5), channel_id=1, replica_groups=mesh['x'=4,'z'=8,'y'=4,'c'=2] {'x','y'}, dimensions={0} | all-to-all | bytes 2097152 | tf_op jit(solution)/shard_map/all_to_all | solution.py:30
  153.7 4.7 %input_terms.1 = bf16[4,512,512]{2,1,0:T(8,128)(2,1)} custom-call(bf16[512,256]{1,0:T(8,128)(2,1)} %bitcast.102, bf16[512,256]{1,0:T(8,128)(2,1)} %copy-done.13, bf16[4,512,512]{2,1,0:T(8,128)(2,1)} %get-tuple-element.61.w_ref), custom_call_target="tpu_custom_call" | custom-call | tf_op jit(solution)/shard_map/input_terms/pallas_call | solution.py:371
  158.5 5.1 %all-to-all-start.4 = ((bf16[16,2,64,512]{3,2,1,0:T(8,128)(2,1)}), bf16[16,2,64,512]{3,2,1,0:T(8,128)(2,1)S(1)}, u32[]{:S(2)}, u32[]{:S(2)}) async-start(bf16[16,2,64,512]{3,2,1,0:T(8,128)(2,1)} %bitcast.99), calls=%async_computation.4 | async-start | bytes 4194304 | tf_op jit(solution)/shard_map/all_to_all | solution.py:30
  165.7 4.7 %collective-permute-done.28 = bf16[256,256]{1,0:T(8,128)(2,1)S(1)} collective-permute-done((bf16[256,256]{1,0:T(8,128)(2,1)S(1)}, bf16[256,256]{1,0:T(8,128)(2,1)S(1)}, u32[]{:S(2)}, u32[]{:S(2)}) %collective-permute-start.28) | collective-permute-done | bytes 131104 | tf_op jit(solution)/shard_map/ppermute | solution.py:26
  170.4 4.5 %weight_terms.1 = bf16[8,528,256]{2,1,0:T(8,128)(2,1)} custom-call(s32[2]{0:T(128)} %pad_add_fusion.place_ref, bf16[4,512,512]{2,1,0:T(8,128)(2,1)} %get-tuple-element.52.own_ref, bf16[4,512,512]{2,1,0:T(8,128)(2,1)} %get-tuple-element.53.oth_ref, bf16[512,256]{1,0:T(8,128)(2,1)} %bitcast.103, f32[1,1]{1,0:T(1,128)} %bitcast.22.share_ref), custom_call_target="tpu_custom_call" | custom-call | tf_op jit(solution)/shard_map/weight_terms/pallas_call | solution.py:383
  179.3 5.6 %collective-permute-done.30 = bf16[528,256]{1,0:T(8,128)(2,1)S(1)} collective-permute-done((bf16[528,256]{1,0:T(8,128)(2,1)S(1)}, bf16[528,256]{1,0:T(8,128)(2,1)S(1)}, u32[]{:S(2)}, u32[]{:S(2)}) %collective-permute-start.30) | collective-permute-done | bytes 270368 | tf_op jit(solution)/shard_map/ppermute | solution.py:26
  189.4 4.7 %collective-permute-done.32 = bf16[528,256]{1,0:T(8,128)(2,1)S(1)} collective-permute-done((bf16[528,256]{1,0:T(8,128)(2,1)S(1)}, bf16[528,256]{1,0:T(8,128)(2,1)S(1)}, u32[]{:S(2)}, u32[]{:S(2)}) %collective-permute-start.32) | collective-permute-done | bytes 270368 | tf_op jit(solution)/shard_map/ppermute | solution.py:26
  198.6 4.4 %collective-permute-done.34 = bf16[528,256]{1,0:T(8,128)(2,1)S(1)} collective-permute-done((bf16[528,256]{1,0:T(8,128)(2,1)S(1)}, bf16[528,256]{1,0:T(8,128)(2,1)S(1)}, u32[]{:S(2)}, u32[]{:S(2)}) %collective-permute-start.34) | collective-permute-done | bytes 270368 | tf_op jit(solution)/shard_map/ppermute | solution.py:26
  204.8 4.2 %all-to-all-start.5 = ((bf16[4,128,256]{2,1,0:T(8,128)(2,1)}), bf16[4,128,256]{2,1,0:T(8,128)(2,1)S(1)}, u32[]{:S(2)}, u32[]{:S(2)}) async-start(bf16[4,128,256]{2,1,0:T(8,128)(2,1)} %bitcast.30), calls=%async_computation.5 | async-start | bytes 524288 | tf_op jit(solution)/shard_map/all_to_all | solution.py:30
  (170 shorter events, 82.8 us)
Async XLA Ops:
  2.3 11.0 %all-to-all-start = ((bf16[4,128,256]{2,1,0:T(8,128)(2,1)}), bf16[4,128,256]{2,1,0:T(8,128)(2,1)S(1)}, u32[]{:S(2)}, u32[]{:S(2)}) async-start(bf16[4,128,256]{2,1,0:T(8,128)(2,1)} %pad_maximum_fusion), calls=%async_computation | async-start | bytes 524288 | tf_op jit(solution)/shard_map/all_to_all | solution.py:30
  14.9 34.5 %all-to-all-start.1 = ((bf16[16,2,64,512]{3,2,1,0:T(8,128)(2,1)}), bf16[16,2,64,512]{3,2,1,0:T(8,128)(2,1)S(1)}, u32[]{:S(2)}, u32[]{:S(2)}) async-start(bf16[16,2,64,512]{3,2,1,0:T(8,128)(2,1)} %broadcast_in_dim.4), calls=%async_computation.1 | async-start | bytes 4194304 | tf_op jit(solution)/shard_map/all_to_all | solution.py:30
  20.4 9.7 %collective-permute-start = (bf16[4,128,256]{2,1,0:T(8,128)(2,1)S(1)}, bf16[4,128,256]{2,1,0:T(8,128)(2,1)S(1)}, u32[]{:S(2)}, u32[]{:S(2)}) collective-permute-start(bf16[4,128,256]{2,1,0:T(8,128)(2,1)S(1)} %all-to-all-done.refs_0_), channel_id=1, source_target_pairs={{0,56},{8,0},{16,8},{24,16},{32,24},{40,32},{48,40},{56,48},{1,57}... | collective-permute-start | bytes 786440 | tf_op jit(solution)/shard_map/ppermute | solution.py:26
  33.8 7.9 %collective-permute-start.4 = (bf16[4,128,256]{2,1,0:T(8,128)(2,1)S(1)}, bf16[4,128,256]{2,1,0:T(8,128)(2,1)S(1)}, u32[]{:S(2)}, u32[]{:S(2)}) collective-permute-start(bf16[4,128,256]{2,1,0:T(8,128)(2,1)S(1)} %collective-permute-done.3.refs_6_), channel_id=1, source_target_pairs={{0,8},{8,16},{16,24},{24,32},{32,40},{40,48},{48,56},{56,0},{1,9},... | collective-permute-start | bytes 786440 | tf_op jit(solution)/shard_map/ppermute | solution.py:26
  49.3 8.9 %collective-permute-start.6 = (bf16[4,4,2,64,512]{4,3,2,1,0:T(8,128)(2,1)S(1)}, bf16[4,4,2,64,512]{4,3,2,1,0:T(8,128)(2,1)}, u32[]{:S(2)}, u32[]{:S(2)}) collective-permute-start(bf16[4,4,2,64,512]{4,3,2,1,0:T(8,128)(2,1)S(1)} %bitcast.96), channel_id=1, source_target_pairs={{0,1},{1,0},{2,3},{3,2},{4,5},{5,4},{6,7},{7,6},{8,9},{9,8},{10,11... | collective-permute-start | bytes 6291464 | tf_op jit(solution)/shard_map/ppermute | solution.py:22
  50.3 8.0 %collective-permute-start.7 = (bf16[2,128,256]{2,1,0:T(8,128)(2,1)}, bf16[2,128,256]{2,1,0:T(8,128)(2,1)S(1)}, u32[]{:S(2)}, u32[]{:S(2)}) collective-permute-start(bf16[2,128,256]{2,1,0:T(8,128)(2,1)} %slice.141), channel_id=1, source_target_pairs={{0,8},{8,16},{16,24},{24,32},{32,40},{40,48},{48,56},{56,0},{1,9},... | collective-permute-start | bytes 393224 | tf_op jit(solution)/shard_map/ppermute | solution.py:26
  66.7 9.3 %collective-permute-start.11 = (bf16[128,512]{1,0:T(8,128)(2,1)S(1)}, bf16[128,512]{1,0:T(8,128)(2,1)S(1)}, u32[]{:S(2)}, u32[]{:S(2)}) collective-permute-start(bf16[128,512]{1,0:T(8,128)(2,1)S(1)} %slice.144.refs_1_), channel_id=1, source_target_pairs={{0,56},{8,0},{16,8},{24,16},{32,24},{40,32},{48,40},{56,48},{1,57}... | collective-permute-start | bytes 393224 | tf_op jit(solution)/shard_map/ppermute | solution.py:26
  74.0 7.8 %collective-permute-start.17 = (bf16[144,512]{1,0:T(8,128)(2,1)S(1)}, bf16[144,512]{1,0:T(8,128)(2,1)S(1)}, u32[]{:S(2)}, u32[]{:S(2)}) collective-permute-start(bf16[144,512]{1,0:T(8,128)(2,1)S(1)} %collective-permute-done.16.refs_14_), channel_id=1, source_target_pairs={{0,8},{8,16},{16,24},{24,32},{32,40},{40,48},{48,56},{56,0},{1,9},... | collective-permute-start | bytes 442376 | tf_op jit(solution)/shard_map/ppermute | solution.py:26
  74.0 9.6 %collective-permute-start.21 = (bf16[128,512]{1,0:T(8,128)(2,1)S(1)}, bf16[128,512]{1,0:T(8,128)(2,1)S(1)}, u32[]{:S(2)}, u32[]{:S(2)}) collective-permute-start(bf16[128,512]{1,0:T(8,128)(2,1)S(1)} %slice.144.refs_1_), channel_id=1, source_target_pairs={{0,8},{8,16},{16,24},{24,32},{32,40},{40,48},{48,56},{56,0},{1,9},... | collective-permute-start | bytes 393224 | tf_op jit(solution)/shard_map/ppermute | solution.py:26
  77.6 12.4 %collective-permute-start.12 = (bf16[144,512]{1,0:T(8,128)(2,1)S(1)}, bf16[144,512]{1,0:T(8,128)(2,1)S(1)}, u32[]{:S(2)}, u32[]{:S(2)}) collective-permute-start(bf16[144,512]{1,0:T(8,128)(2,1)S(1)} %collective-permute-done.10.refs_2_), channel_id=1, source_target_pairs={{0,56},{8,0},{16,8},{24,16},{32,24},{40,32},{48,40},{56,48},{1,57}... | collective-permute-start | bytes 442376 | tf_op jit(solution)/shard_map/ppermute | solution.py:26
  81.8 11.6 %collective-permute-start.18 = (bf16[144,512]{1,0:T(8,128)(2,1)S(1)}, bf16[144,512]{1,0:T(8,128)(2,1)S(1)}, u32[]{:S(2)}, u32[]{:S(2)}) collective-permute-start(bf16[144,512]{1,0:T(8,128)(2,1)S(1)} %collective-permute-done.17.refs_12_), channel_id=1, source_target_pairs={{0,8},{8,16},{16,24},{24,32},{32,40},{40,48},{48,56},{56,0},{1,9},... | collective-permute-start | bytes 442376 | tf_op jit(solution)/shard_map/ppermute | solution.py:26
  83.6 9.7 %collective-permute-start.15 = (bf16[128,512]{1,0:T(8,128)(2,1)S(1)}, bf16[128,512]{1,0:T(8,128)(2,1)S(1)}, u32[]{:S(2)}, u32[]{:S(2)}) collective-permute-start(bf16[128,512]{1,0:T(8,128)(2,1)S(1)} %collective-permute-done.13.refs_5_), channel_id=1, source_target_pairs={{0,56},{8,0},{16,8},{24,16},{32,24},{40,32},{48,40},{56,48},{1,57}... | collective-permute-start | bytes 393224 | tf_op jit(solution)/shard_map/ppermute | solution.py:26
  86.9 25.4 %collective-permute-start.25 = (bf16[4,512,256]{2,1,0:T(8,128)(2,1)}, bf16[4,512,256]{2,1,0:T(8,128)(2,1)S(1)}, u32[]{:S(2)}, u32[]{:S(2)}) collective-permute-start(bf16[4,512,256]{2,1,0:T(8,128)(2,1)} %get-tuple-element.48), channel_id=1, source_target_pairs={{0,1},{1,0},{2,3},{3,2},{4,5},{5,4},{6,7},{7,6},{8,9},{9,8},{10,11... | collective-permute-start | bytes 3145736 | tf_op jit(solution)/shard_map/ppermute | solution.py:22
  90.1 8.4 %collective-permute-start.23 = (bf16[128,512]{1,0:T(8,128)(2,1)S(1)}, bf16[128,512]{1,0:T(8,128)(2,1)S(1)}, u32[]{:S(2)}, u32[]{:S(2)}) collective-permute-start(bf16[128,512]{1,0:T(8,128)(2,1)S(1)} %collective-permute-done.22.refs_13_), channel_id=1, source_target_pairs={{0,8},{8,16},{16,24},{24,32},{32,40},{40,48},{48,56},{56,0},{1,9},... | collective-permute-start | bytes 393224 | tf_op jit(solution)/shard_map/ppermute | solution.py:26
  90.1 8.4 %collective-permute-start.14 = (bf16[144,512]{1,0:T(8,128)(2,1)S(1)}, bf16[144,512]{1,0:T(8,128)(2,1)S(1)}, u32[]{:S(2)}, u32[]{:S(2)}) collective-permute-start(bf16[144,512]{1,0:T(8,128)(2,1)S(1)} %collective-permute-done.12.refs_4_), channel_id=1, source_target_pairs={{0,56},{8,0},{16,8},{24,16},{32,24},{40,32},{48,40},{56,48},{1,57}... | collective-permute-start | bytes 442376 | tf_op jit(solution)/shard_map/ppermute | solution.py:26
  104.3 20.8 %all-to-all-start.2 = ((bf16[16,16,2176]{2,1,0:T(8,128)(2,1)}), bf16[16,16,2176]{2,1,0:T(8,128)(2,1)S(1)}, u32[]{:S(2)}, u32[]{:S(2)}) async-start(bf16[16,16,2176]{2,1,0:T(8,128)(2,1)} %bitcast.105), calls=%async_computation.2 | async-start | bytes 2228224 | tf_op jit(solution)/shard_map/all_to_all | solution.py:30
  153.0 17.4 %collective-permute-start.29 = (bf16[272,256]{1,0:T(8,128)(2,1)}, bf16[272,256]{1,0:T(8,128)(2,1)S(1)}, u32[]{:S(2)}, u32[]{:S(2)}) collective-permute-start(bf16[272,256]{1,0:T(8,128)(2,1)} %get-tuple-element.59), channel_id=1, source_target_pairs={{0,56},{8,0},{16,8},{24,16},{32,24},{40,32},{48,40},{56,48},{1,57}... | collective-permute-start | bytes 417800 | tf_op jit(solution)/shard_map/ppermute | solution.py:26
  158.5 46.4 %all-to-all-start.4 = ((bf16[16,2,64,512]{3,2,1,0:T(8,128)(2,1)}), bf16[16,2,64,512]{3,2,1,0:T(8,128)(2,1)S(1)}, u32[]{:S(2)}, u32[]{:S(2)}) async-start(bf16[16,2,64,512]{3,2,1,0:T(8,128)(2,1)} %bitcast.99), calls=%async_computation.4 | async-start | bytes 4194304 | tf_op jit(solution)/shard_map/all_to_all | solution.py:30
  176.0 8.9 %collective-permute-start.30 = (bf16[528,256]{1,0:T(8,128)(2,1)S(1)}, bf16[528,256]{1,0:T(8,128)(2,1)S(1)}, u32[]{:S(2)}, u32[]{:S(2)}) collective-permute-start(bf16[528,256]{1,0:T(8,128)(2,1)S(1)} %get-tuple-element.81), channel_id=1, source_target_pairs={{0,8},{8,16},{16,24},{24,32},{32,40},{40,48},{48,56},{56,0},{1,9},... | collective-permute-start | bytes 811016 | tf_op jit(solution)/shard_map/ppermute | solution.py:26
  176.6 8.3 %collective-permute-start.31 = (bf16[528,256]{1,0:T(8,128)(2,1)S(1)}, bf16[528,256]{1,0:T(8,128)(2,1)S(1)}, u32[]{:S(2)}, u32[]{:S(2)}) collective-permute-start(bf16[528,256]{1,0:T(8,128)(2,1)S(1)} %get-tuple-element.80), channel_id=1, source_target_pairs={{0,56},{8,0},{16,8},{24,16},{32,24},{40,32},{48,40},{56,48},{1,57}... | collective-permute-start | bytes 811016 | tf_op jit(solution)/shard_map/ppermute | solution.py:26
  186.1 8.0 %collective-permute-start.32 = (bf16[528,256]{1,0:T(8,128)(2,1)S(1)}, bf16[528,256]{1,0:T(8,128)(2,1)S(1)}, u32[]{:S(2)}, u32[]{:S(2)}) collective-permute-start(bf16[528,256]{1,0:T(8,128)(2,1)S(1)} %get-tuple-element.79), channel_id=1, source_target_pairs={{0,8},{8,16},{16,24},{24,32},{32,40},{40,48},{48,56},{56,0},{1,9},... | collective-permute-start | bytes 811016 | tf_op jit(solution)/shard_map/ppermute | solution.py:26
  186.2 8.0 %collective-permute-start.33 = (bf16[528,256]{1,0:T(8,128)(2,1)S(1)}, bf16[528,256]{1,0:T(8,128)(2,1)S(1)}, u32[]{:S(2)}, u32[]{:S(2)}) collective-permute-start(bf16[528,256]{1,0:T(8,128)(2,1)S(1)} %get-tuple-element.78), channel_id=1, source_target_pairs={{0,56},{8,0},{16,8},{24,16},{32,24},{40,32},{48,40},{56,48},{1,57}... | collective-permute-start | bytes 811016 | tf_op jit(solution)/shard_map/ppermute | solution.py:26
  195.3 7.7 %collective-permute-start.34 = (bf16[528,256]{1,0:T(8,128)(2,1)S(1)}, bf16[528,256]{1,0:T(8,128)(2,1)S(1)}, u32[]{:S(2)}, u32[]{:S(2)}) collective-permute-start(bf16[528,256]{1,0:T(8,128)(2,1)S(1)} %get-tuple-element.76), channel_id=1, source_target_pairs={{0,8},{8,16},{16,24},{24,32},{32,40},{40,48},{48,56},{56,0},{1,9},... | collective-permute-start | bytes 811016 | tf_op jit(solution)/shard_map/ppermute | solution.py:26
  204.8 10.9 %all-to-all-start.5 = ((bf16[4,128,256]{2,1,0:T(8,128)(2,1)}), bf16[4,128,256]{2,1,0:T(8,128)(2,1)S(1)}, u32[]{:S(2)}, u32[]{:S(2)}) async-start(bf16[4,128,256]{2,1,0:T(8,128)(2,1)} %bitcast.30), calls=%async_computation.5 | async-start | bytes 524288 | tf_op jit(solution)/shard_map/all_to_all | solution.py:30
  (50 other events, 487.2 us)
